TPU v7x, 512 devices: a whole 4x8x8 slice. The times are simulated.
512 devices in a mesh: dp: 4 (over y_lo), head: 8 (over z), ctx: 16 (over x, y_hi, core).
Axes of the slice: x: 4, y: 8 (y_hi: 2, y_lo: 4; y = y_hi * 4 + y_lo), z: 8, core: 2. Of those that a mesh axis runs over, the one named last changes fastest.
Arguments:
- query_rows: bfloat16 [16384, 8192], P(('dp', 'ctx'), 'head'), parts along dimension 0, may hold values from -12 to 12
- key_rows: bfloat16 [16384, 1024], P(('dp', 'ctx'), 'head'), parts along dimension 0, may hold values from -4 to 4
- stored_value_rows: bfloat16 [16384, 1024], P(('dp', 'ctx'), 'head'), parts along dimension 0, may hold values from -6 to 6
- out_grad: bfloat16 [16384, 8192], P(('dp', 'ctx'), 'head'), parts along dimension 0, may hold values from -6 to 6
- block_table: int32 [64, 2], P('dp'), parts along dimension 0, may hold values from 0 to 31, as said below
- pattern: int32 [128, 10], P('dp'), parts along dimension 0, may hold values from 0 to 31, as said below
Outputs:
- attended: bfloat16 [16384, 8192], P(('dp', 'ctx'), 'head'), parts along dimension 0
- query_grad: bfloat16 [16384, 8192], P(('dp', 'ctx'), 'head'), parts along dimension 0
- key_grad: bfloat16 [16384, 1024], P(('dp', 'ctx'), 'head'), parts along dimension 0
- value_grad: bfloat16 [16384, 1024], P(('dp', 'ctx'), 'head'), parts along dimension 0
There are 4 independent parts, one for each index of `dp`. A program takes and returns all parts, laid end to end along the dimension named above; each array names one. Nothing has to cross between parts.
Inputs may be any that keep to these rules, and one draw needn't show every extreme that they name: `pattern`: row b lists the key blocks that sequence block b reads, in no order; every entry is at most b; b, max(b - 1, 0) and 0 are always listed; repeated entries count once. `block_table`: each sequence block is held by exactly one storage block, and sequence blocks b and 31 - b are held by the same ctx index.
All inputs are finite; a program needn't handle non-finite values.
Results may differ from a plain program's by a relative error of at most 0.015.
Values may be sent and summed in bfloat16 or wider, within the bound.
No kernel may reach another device: no remote copies, remote signals or barrier semaphores. Data moves between devices by JAX's collectives and lax.ppermute only.
A program may use at most 64 MiB of HBM per device.

v0:
```python
import jax
import jax.numpy as jnp
from jax import lax
from jax.sharding import PartitionSpec as P

HEAD_SIZE = 128
BLK = 128


def slot_layout(block_table, pattern, held_seq):
    blocks = pattern.shape[0]
    slots = pattern.shape[1]
    block_ids = jnp.arange(blocks, dtype=jnp.int32)
    store_seq = block_table.reshape(-1)
    inverse = jnp.sum(
        jnp.where(store_seq[:, None] == block_ids[None, :], block_ids[:, None], 0), axis=0
    )
    onehot = (held_seq[:, None] == block_ids[None, :]).astype(jnp.int32)
    held_pattern = jnp.sum(onehot[:, :, None] * pattern[None, :, :], axis=1)
    key_store = jnp.sum(
        jnp.where(held_pattern[:, :, None] == block_ids[None, None, :], inverse[None, None, :], 0),
        axis=2,
    )
    same = held_pattern[:, :, None] == held_pattern[:, None, :]
    slot_ids = jnp.arange(slots, dtype=jnp.int32)
    before = slot_ids[None, :] < slot_ids[:, None]
    live_slot = jnp.logical_not(jnp.any(same & before[None], axis=2))
    inner = jnp.arange(BLK, dtype=jnp.int32)
    query_pos = held_seq[:, None] * BLK + inner[None, :]
    key_pos = held_pattern[:, :, None] * BLK + inner[None, None, :]
    allowed = live_slot[:, None, :, None] & (key_pos[:, None, :, :] <= query_pos[:, :, None, None])
    return (key_store, allowed)


def attend_tiles(query_held, grad_held, key_tiles, value_tiles, allowed):
    scaling = HEAD_SIZE ** (-0.5)
    scores = (
        jnp.einsum("biagd,bjkad->bagijk", query_held, key_tiles, preferred_element_type=jnp.float32)
        * scaling
    )
    scores = jnp.where(allowed[:, None, None], scores, -jnp.inf)
    row_max = jnp.max(scores, axis=(4, 5), keepdims=True)
    row_sum = jnp.sum(jnp.exp(scores - row_max), axis=(4, 5), keepdims=True)
    log_total = row_max + jnp.log(row_sum)
    prob_full = jnp.exp(scores - log_total)
    prob_low = prob_full.astype(jnp.bfloat16)
    attended_wide = jnp.einsum(
        "bagijk,bjkad->biagd", prob_low, value_tiles, preferred_element_type=jnp.float32
    )
    attended = attended_wide.astype(jnp.bfloat16)
    row_dot = jnp.sum(grad_held.astype(jnp.float32) * attended_wide, axis=-1)
    row_dot = jnp.transpose(row_dot, (0, 2, 3, 1))[..., None, None]
    grad_prob = jnp.einsum(
        "biagd,bjkad->bagijk", grad_held, value_tiles, preferred_element_type=jnp.float32
    )
    grad_score = (prob_full * (grad_prob - row_dot) * scaling).astype(jnp.bfloat16)
    query_grad = jnp.einsum(
        "bagijk,bjkad->biagd", grad_score, key_tiles, preferred_element_type=jnp.float32
    ).astype(jnp.bfloat16)
    key_grads = jnp.einsum(
        "bagijk,biagd->bjkad", grad_score, query_held, preferred_element_type=jnp.float32
    )
    value_grads = jnp.einsum(
        "bagijk,biagd->bjkad", prob_low, grad_held, preferred_element_type=jnp.float32
    )
    return (attended, query_grad, key_grads, value_grads)


def per_device(query_rows, key_rows, stored_value_rows, out_grad, block_table, pattern):
    ctx_index = lax.axis_index("ctx")
    per_dev = block_table.shape[1]
    blocks = pattern.shape[0]
    kv_local = key_rows.shape[1] // HEAD_SIZE
    groups = query_rows.shape[1] // key_rows.shape[1]
    held_rows = per_dev * BLK
    held_seq = lax.dynamic_index_in_dim(block_table, ctx_index, 0, keepdims=False)
    key_store, allowed = slot_layout(block_table, pattern, held_seq)
    key_all, value_all = (
        lax.all_gather(key_rows, "ctx", axis=0, tiled=True),
        lax.all_gather(stored_value_rows, "ctx", axis=0, tiled=True),
    )
    key_blocks = key_all.reshape(blocks, BLK, kv_local, HEAD_SIZE)
    value_blocks = value_all.reshape(blocks, BLK, kv_local, HEAD_SIZE)
    key_tiles = key_blocks[key_store]
    value_tiles = value_blocks[key_store]
    query_held = query_rows.reshape(per_dev, BLK, kv_local, groups, HEAD_SIZE)
    grad_held = out_grad.reshape(per_dev, BLK, kv_local, groups, HEAD_SIZE)
    attended, query_grad, key_grads, value_grads = attend_tiles(
        query_held, grad_held, key_tiles, value_tiles, allowed
    )
    flat_slots = key_store.reshape(-1)
    key_partial = (
        jnp.zeros((blocks, BLK, kv_local, HEAD_SIZE), jnp.float32)
        .at[flat_slots]
        .add(key_grads.reshape(-1, BLK, kv_local, HEAD_SIZE))
    )
    value_partial = (
        jnp.zeros((blocks, BLK, kv_local, HEAD_SIZE), jnp.float32)
        .at[flat_slots]
        .add(value_grads.reshape(-1, BLK, kv_local, HEAD_SIZE))
    )
    key_sum, value_sum = (
        lax.psum_scatter(
            key_partial.reshape(blocks * BLK, -1).astype(jnp.bfloat16),
            "ctx",
            scatter_dimension=0,
            tiled=True,
        ).astype(jnp.float32),
        lax.psum_scatter(
            value_partial.reshape(blocks * BLK, -1).astype(jnp.bfloat16),
            "ctx",
            scatter_dimension=0,
            tiled=True,
        ).astype(jnp.float32),
    )
    attended = attended.reshape(held_rows, -1)
    query_grad = query_grad.reshape(held_rows, -1)
    key_grad = key_sum.astype(jnp.bfloat16)
    value_grad = value_sum.astype(jnp.bfloat16)
    return (attended, query_grad, key_grad, value_grad)


def solution(mesh):
    in_specs = (
        P(("dp", "ctx"), "head"),
        P(("dp", "ctx"), "head"),
        P(("dp", "ctx"), "head"),
        P(("dp", "ctx"), "head"),
        P("dp", None),
        P("dp", None),
    )
    out_specs = (
        P(("dp", "ctx"), "head"),
        P(("dp", "ctx"), "head"),
        P(("dp", "ctx"), "head"),
        P(("dp", "ctx"), "head"),
    )
    return jax.shard_map(
        per_device, mesh=mesh, in_specs=in_specs, out_specs=out_specs, check_vma=False
    )
```

profile of v0, /device:TPU:6, one launch (start us, length us, event | category | flops | bytes accessed | tf_op | source)
XLA Modules:
  0.0 322.1 jit_solution(11498761475473287322)
XLA Ops:
  12.6 1.1 copy.98
  13.8 1.1 convert_bitcast_fusion
  14.9 1.1 copy.100
  17.1 1.4 copy.65
  19.0 54.9 %all-gather.5.cloned.1.call-done = bf16[4096,128]{1,0:T(8,128)(2,1)} async-done(((bf16[256,128]{1,0:T(8,128)(2,1)}), bf16[4096,128]{1,0:T(8,128)(2,1)}) %all-gather.5.cloned.1.call-update) | async-done | bytes 1048592 | tf_op jit(solution)/shard_map/all_gather | solution.py:79
  73.8 1.9 gather_fusion.1
  75.8 1.5 fusion.4
  77.3 2.3 exponential_reduce_fusion
  79.6 2.5 fusion.9
  82.2 1.5 broadcast.134.clone.1
  83.7 5.9 %scatter_fusion.1 = f32[32,128,128]{2,1,0:T(8,128)} fusion(f32[32,128,128]{2,1,0:T(8,128)} %broadcast.134.clone.1, s32[20]{0:T(128)S(1)} %fusion.17, f32[20,128,128]{2,1,0:T(8,128)S(1)} %bitcast.169), kind=kCustom, calls=%fused_computation.3 | custom fusion | flops 327680 | bytes 3932240 | tf_op jit(solution)/shard_map/scatter-add | solution.py:100
  89.6 3.0 convert_element_type.70
  92.8 41.1 %all-gather.3.cloned.1.call-done = bf16[4096,128]{1,0:T(8,128)(2,1)} async-done(((bf16[256,128]{1,0:T(8,128)(2,1)}), bf16[4096,128]{1,0:T(8,128)(2,1)}) %all-gather.3.cloned.1.call-update) | async-done | bytes 1048592 | tf_op jit(solution)/shard_map/all_gather | solution.py:80
  134.0 2.8 gather_fusion
  136.7 8.0 %multiply_reduce_fusion = (f32[2,128,8]{1,2,0:T(8,128)S(1)}, bf16[2,128,1,8,128]{1,4,3,0,2:T(8,128)(2,1)}) fusion(f32[2,128,1,8,128]{1,4,3,0,2:T(8,128)} %copy.65, bf16[2,10,128,128,1]{3,2,4,1,0:T(8,128)(2,1)} %bitcast.170, f32[2,10,128,128,8]{3,2,4,1,0:T(8,128)} %copy-done, f32[2,8,128]{2,1,0:T(8,128)S(1)} %log_add_fusion, ...), kind=kOutput, calls=%fused_computation.21 | convolution fusion | flops 682358784 | bytes 13058048 | tf_op jit(solution)/shard_map/bagijk,bjkad->biagd/dot_general | solution.py:47
  144.8 3.6 %fusion.6 = bf16[2,8,128,10,128]{2,4,1,3,0:T(8,128)(2,1)S(1)} fusion(f32[2,10,128,128,8]{3,2,4,1,0:T(8,128)S(1)} %bitcast.157, f32[2,8,128]{2,1,0:T(8,128)S(1)} %bitcast.175, f32[2,8,128]{2,1,0:T(8,128)S(1)} %log_add_fusion, pred[2,128,10,128]{1,3,2,0:T(8,128)(4,1)S(1)} %copy-done.3, bf16[2,10,128,128,1]{3,2,4,1,0:T(8,128)(2,1)S(1)} %bitcast.171, ...), kind=kOutput, calls=%fused_computation.14 | convolution fusion | flops 689438720 | bytes 17252352 | tf_op jit(solution)/shard_map/biagd,bjkad->bagijk/dot_general | solution.py:53
  148.4 2.3 copy-done.1
  150.7 2.6 fusion.12
  153.6 4.4 %scatter_fusion = f32[32,128,128]{2,1,0:T(8,128)S(1)} fusion(f32[32,128,128]{2,1,0:T(8,128)S(1)} %broadcast.134.clone, s32[20]{0:T(128)S(1)} %fusion.17, f32[20,128,128]{2,1,0:T(8,128)} %bitcast.160), kind=kCustom, calls=%fused_computation.2 | custom fusion | flops 327680 | bytes 3932240 | tf_op jit(solution)/shard_map/scatter-add | solution.py:95
  158.0 1.2 convert_element_type.69
  159.2 3.5 %fusion.8 = bf16[2,128,1,8,128]{1,4,3,0,2:T(8,128)(2,1)S(1)} fusion(bf16[2,10,128,128,1]{3,2,4,1,0:T(8,128)(2,1)S(1)} %bitcast.159, bf16[2,8,128,10,128]{2,4,1,3,0:T(8,128)(2,1)} %copy-done.1), kind=kOutput, calls=%fused_computation.19 | convolution fusion | flops 671350784 | bytes 6422528 | tf_op jit(solution)/shard_map/bagijk,bjkad->biagd/dot_general | solution.py:57
  163.3 1.2 copy_bitcast_fusion
  164.5 60.9 %reduce-scatter.5.cloned.1.call-done = bf16[256,128]{1,0:T(8,128)(2,1)} async-done(((bf16[4096,128]{1,0:T(8,128)(2,1)}), bf16[256,128]{1,0:T(8,128)(2,1)}) %reduce-scatter.5.cloned.1.call-update) | async-done | bytes 65552 | tf_op jit(solution)/shard_map/reduce_scatter | solution.py:109
  225.4 90.2 %reduce-scatter.3.cloned.1.call-done = bf16[256,128]{1,0:T(8,128)(2,1)} async-done(((bf16[4096,128]{1,0:T(8,128)(2,1)}), bf16[256,128]{1,0:T(8,128)(2,1)}) %reduce-scatter.3.cloned.1.call-update) | async-done | bytes 65552 | tf_op jit(solution)/shard_map/reduce_scatter | solution.py:103
  (59 shorter events, 8.1 us)
Async XLA Ops:
  7.2 66.7 %all-gather.5.cloned.1.call-start = ((), (), s32[]{:S(2)}) async-start(), calls=%async_computation.3 | async-start | bytes 1114112 | tf_op jit(solution)/shard_map/all_gather | solution.py:79
  7.9 126.1 %all-gather.3.cloned.1.call-start = ((), (), s32[]{:S(2)}) async-start(), calls=%async_computation.2 | async-start | bytes 1114112 | tf_op jit(solution)/shard_map/all_gather | solution.py:80
  8.6 216.8 %reduce-scatter.5.cloned.1.call-start = ((), (), s32[]{:S(2)}) async-start(), calls=%async_computation.5 | async-start | bytes 1114112 | tf_op jit(solution)/shard_map/reduce_scatter | solution.py:109
  19.0 64.7 %copy-start.2 = (pred[2,128,10,128]{1,3,2,0:T(8,128)(4,1)}, pred[2,128,10,128]{1,3,2,0:T(8,128)(4,1)S(1)}, u32[]{:S(2)}) copy-start(pred[2,128,10,128]{1,3,2,0:T(8,128)(4,1)S(1)} %compare_and_fusion) | copy-start | bytes 983044
  75.8 3.9 %copy-start.5 = (bf16[2,128,8,128,1]{3,2,1,0,4:T(8,128)(2,1)S(1)}, bf16[2,128,8,128,1]{3,2,1,0,4:T(8,128)(2,1)}, u32[]{:S(2)}) copy-start(bf16[2,128,8,128,1]{3,2,1,0,4:T(8,128)(2,1)} %bitcast_bitcast_fusion) | copy-start | bytes 1572868
  77.3 4.9 %copy-start = (f32[2,10,128,128,8]{3,2,4,1,0:T(8,128)}, f32[2,10,128,128,8]{3,2,4,1,0:T(8,128)S(1)}, u32[]{:S(2)}) copy-start(f32[2,10,128,128,8]{3,2,4,1,0:T(8,128)S(1)} %get-tuple-element.7) | copy-start | bytes 31457284
  89.6 55.1 %slice-start = ((s8[10485760]{0:T(1024)(128)(4,1)}), s8[2097152]{0:T(1024)(128)(4,1)S(1)}, s32[]{:S(2)}) async-start(s8[10485760]{0:T(1024)(128)(4,1)} %bitcast.156), calls=%async_computation.6 | async-start | bytes 4194304
  92.6 222.9 %reduce-scatter.3.cloned.1.call-start = ((), (), s32[]{:S(2)}) async-start(), calls=%async_computation.4 | async-start | bytes 1114112 | tf_op jit(solution)/shard_map/reduce_scatter | solution.py:103
  136.7 8.0 %copy-start.3 = (pred[2,128,10,128]{1,3,2,0:T(8,128)(4,1)S(1)}, pred[2,128,10,128]{1,3,2,0:T(8,128)(4,1)}, u32[]{:S(2)}) copy-start(pred[2,128,10,128]{1,3,2,0:T(8,128)(4,1)} %copy-done.2) | copy-start | bytes 983044
  136.7 8.0 %copy-start.4 = (bf16[20,128,128]{2,1,0:T(8,128)(2,1)S(1)}, bf16[20,128,128]{2,1,0:T(8,128)(2,1)}, u32[]{:S(2)}) copy-start(bf16[20,128,128]{2,1,0:T(8,128)(2,1)} %gather_fusion) | copy-start | bytes 1966084
  136.7 8.0 %copy-start.6 = (bf16[2,128,8,128,1]{3,2,1,0,4:T(8,128)(2,1)S(1)}, bf16[2,128,8,128,1]{3,2,1,0,4:T(8,128)(2,1)}, u32[]{:S(2)}) copy-start(bf16[2,128,8,128,1]{3,2,1,0,4:T(8,128)(2,1)} %bitcast_bitcast_fusion) | copy-start | bytes 1572868
  136.7 8.0 %slice-start.1 = ((s8[10485760]{0:T(1024)(128)(4,1)}), s8[4194304]{0:T(1024)(128)(4,1)S(1)}, s32[]{:S(2)}) async-start(s8[10485760]{0:T(1024)(128)(4,1)} %bitcast.156), calls=%async_computation.7 | async-start | bytes 8388608
  136.7 8.0 %slice-start.2 = ((s8[10485760]{0:T(1024)(128)(4,1)}), s8[4194304]{0:T(1024)(128)(4,1)S(1)}, s32[]{:S(2)}) async-start(s8[10485760]{0:T(1024)(128)(4,1)} %bitcast.156), calls=%async_computation.8 | async-start | bytes 8388608
  148.4 2.3 copy-start.1
  153.3 9.7 %copy-start.7 = (bf16[2,128,1,8,128]{1,4,3,0,2:T(8,128)(2,1)S(1)}, bf16[2,128,1,8,128]{1,4,3,0,2:T(8,128)(2,1)}, u32[]{:S(2)}) copy-start(bf16[2,128,1,8,128]{1,4,3,0,2:T(8,128)(2,1)} %get-tuple-element.5) | copy-start | bytes 1572868
Sparse Core Ops, SparseCore 0:
  11.3 62.5 all-gather.4
  77.1 56.8 all-gather.2
  139.2 86.1 reduce-scatter.4
  231.2 84.2 reduce-scatter.2
where the time goes:
time: 323 us; the launch traced here: 322 us
  waiting for transfers between devices  248 us (77%)
  matrix products  21.8 us (7%)
  other arithmetic  20.2 us (6%)
  local copies, waits for them, and re-layouts  17.3 us (5%)
  between operations  14 us (4%)
    reduce_scatter x1, waiting for transfers between devices, per_device(): lax.psum_scatter(key_partial.reshape(blocks * BLK, -1).astype(jnp.bfloat1...  90.2 us
    reduce_scatter x1, waiting for transfers between devices, per_device(): lax.psum_scatter(value_partial.reshape(blocks * BLK, -1).astype(jnp.bfloa...  60.9 us
    all_gather x1, waiting for transfers between devices, per_device(): lax.all_gather(key_rows, 'ctx', axis=0, tiled=True)  54.9 us
    all_gather x1, waiting for transfers between devices, per_device(): lax.all_gather(stored_value_rows, 'ctx', axis=0, tiled=True)  41.1 us
    dot_general x1, matrix products, attend_tiles(): jnp.einsum('bagijk,bjkad->biagd', prob_low, value_tiles, preferred_elemen...  7.98 us
  transfers between devices with their start and end apart: 4, of which 4 were waited for; matrix products, arithmetic and copies ran while one was open for 18% of the time, Pallas kernels for 0%

commit v1 on v0

v1 whole, which is shorter than its diff:
```python
import math

import jax
import jax.numpy as jnp
from jax import lax
from jax.experimental import pallas as pl
from jax.experimental.pallas import tpu as pltpu
from jax.sharding import Mesh, PartitionSpec as P

D = 128
BLK = 128
NX, NY, NC = 4, 2, 2
NEG = -1e30
SWAP = [(0, 1), (1, 0)]


def slot_tables(block_table, pattern, held_seq, my_y, my_core):
    blocks = pattern.shape[0]
    slots = pattern.shape[1]
    block_ids = jnp.arange(blocks, dtype=jnp.int32)
    store_seq = block_table.reshape(-1)
    inverse = jnp.sum(
        jnp.where(store_seq[:, None] == block_ids[None, :], block_ids[:, None], 0), axis=0
    )
    onehot = (held_seq[:, None] == block_ids[None, :]).astype(jnp.int32)
    held_pattern = jnp.sum(onehot[:, :, None] * pattern[None, :, :], axis=1)
    store = jnp.sum(
        jnp.where(held_pattern[:, :, None] == block_ids[None, None, :], inverse[None, None, :], 0),
        axis=2,
    )
    same = held_pattern[:, :, None] == held_pattern[:, None, :]
    slot_ids = jnp.arange(slots, dtype=jnp.int32)
    before = slot_ids[None, :] < slot_ids[:, None]
    live = jnp.logical_not(jnp.any(same & before[None], axis=2)).astype(jnp.int32)
    diag = (held_pattern == held_seq[:, None]).astype(jnp.int32)
    sub = store % 2
    dev = store // 2
    core = dev % 2
    yh = (dev // 2) % 2
    xi = dev // 4
    half = jnp.bitwise_xor(core, my_core)
    row = xi * 1024 + jnp.bitwise_xor(yh, my_y) * 512 + sub * BLK
    kind = live * (1 + diag)
    return jnp.concatenate([half.reshape(-1), row.reshape(-1), kind.reshape(-1)]).astype(jnp.int32)


def attend_kernel(
    tab, q_ref, g_ref, kva_ref, kvb_ref,
    att_ref, qg_ref, pa_ref, pb_ref,
    kg, vg, bias, p_sc, ds_sc, qs, gs, acc_a, acc_b,
):
    nslot = kg.shape[0] // BLK
    heads = q_ref.shape[1] // D
    scale = D ** -0.5
    c2 = scale * math.log2(math.e)
    per = q_ref.shape[0] // BLK
    ns = per * nslot
    acc_a[...] = jnp.zeros_like(acc_a)
    acc_b[...] = jnp.zeros_like(acc_b)

    def one_block(b, _):
        r0 = pl.multiple_of(b * BLK, BLK)
        for j in range(nslot):
            t = b * nslot + j
            half = tab[t]
            row = pl.multiple_of(tab[ns + t], BLK)
            kind = tab[2 * ns + t]
            dst = pl.ds(j * BLK, BLK)

            @pl.when(half == 0)
            def _():
                kg[dst, :] = kva_ref[pl.ds(row, BLK), :]
                vg[dst, :] = kva_ref[pl.ds(row + 256, BLK), :]

            @pl.when(half == 1)
            def _():
                kg[dst, :] = kvb_ref[pl.ds(row, BLK), :]
                vg[dst, :] = kvb_ref[pl.ds(row + 256, BLK), :]

            ri = lax.broadcasted_iota(jnp.int32, (BLK, BLK), 0)
            ci = lax.broadcasted_iota(jnp.int32, (BLK, BLK), 1)
            ok = jnp.logical_or(ci <= ri, kind != 2)
            ok = jnp.logical_and(ok, kind > 0)
            bias[:, j * BLK:(j + 1) * BLK] = jnp.where(ok, 0.0, NEG)

        def one_head(h, _):
            h0 = pl.multiple_of(h * D, D)
            q = q_ref[pl.ds(r0, BLK), pl.ds(h0, D)]
            g = g_ref[pl.ds(r0, BLK), pl.ds(h0, D)]
            qs[pl.ds(h0, BLK), :] = q
            gs[pl.ds(h0, BLK), :] = g
            k = kg[...]
            v = vg[...]
            nt = (((1,), (1,)), ((), ()))
            s = lax.dot_general(q, k, nt, preferred_element_type=jnp.float32)
            s = s * c2 + bias[...]
            m = jnp.max(s, axis=1, keepdims=True)
            e = jnp.exp2(s - m)
            inv = 1.0 / jnp.sum(e, axis=1, keepdims=True)
            prob = e * inv
            low = prob.astype(jnp.bfloat16)
            p_sc[pl.ds(h0, BLK), :] = low
            wide = jnp.dot(low, v, preferred_element_type=jnp.float32)
            att_ref[pl.ds(r0, BLK), pl.ds(h0, D)] = wide.astype(jnp.bfloat16)
            rd = jnp.sum(g.astype(jnp.float32) * wide, axis=1, keepdims=True)
            gp = lax.dot_general(g, v, nt, preferred_element_type=jnp.float32)
            ds = (prob * ((gp - rd) * scale)).astype(jnp.bfloat16)
            ds_sc[pl.ds(h0, BLK), :] = ds
            qg = jnp.dot(ds, k, preferred_element_type=jnp.float32)
            qg_ref[pl.ds(r0, BLK), pl.ds(h0, D)] = qg.astype(jnp.bfloat16)
            return 0

        lax.fori_loop(0, heads, one_head, 0)
        tn = (((0,), (0,)), ((), ()))
        for j0 in range(0, nslot, 2):
            w = pl.ds(j0 * BLK, 2 * BLK)
            dk = lax.dot_general(ds_sc[:, w], qs[...], tn, preferred_element_type=jnp.float32)
            dv = lax.dot_general(p_sc[:, w], gs[...], tn, preferred_element_type=jnp.float32)
            for i in range(2):
                t = b * nslot + j0 + i
                half = tab[t]
                row = pl.multiple_of(tab[ns + t], BLK)
                rows_k = pl.ds(row, BLK)
                rows_v = pl.ds(row + 256, BLK)
                dk_i = dk[i * BLK:(i + 1) * BLK]
                dv_i = dv[i * BLK:(i + 1) * BLK]

                @pl.when(half == 0)
                def _():
                    acc_a[rows_k, :] += dk_i
                    acc_a[rows_v, :] += dv_i

                @pl.when(half == 1)
                def _():
                    acc_b[rows_k, :] += dk_i
                    acc_b[rows_v, :] += dv_i
        return 0

    lax.fori_loop(0, per, one_block, 0)
    pa_ref[...] = acc_a[...].astype(jnp.bfloat16)
    pb_ref[...] = acc_b[...].astype(jnp.bfloat16)


def attend(tab, q, g, kva, kvb, nslot):
    rows, cols = q.shape
    heads = cols // D
    half_rows = kva.shape[0]
    bf = jnp.bfloat16
    vm = pl.BlockSpec(memory_space=pltpu.VMEM)
    return pl.pallas_call(
        attend_kernel,
        out_shape=(
            jax.ShapeDtypeStruct((rows, cols), bf),
            jax.ShapeDtypeStruct((rows, cols), bf),
            jax.ShapeDtypeStruct((half_rows, D), bf),
            jax.ShapeDtypeStruct((half_rows, D), bf),
        ),
        in_specs=[pl.BlockSpec(memory_space=pltpu.SMEM), vm, vm, vm, vm],
        out_specs=(vm, vm, vm, vm),
        scratch_shapes=[
            pltpu.VMEM((nslot * BLK, D), bf),
            pltpu.VMEM((nslot * BLK, D), bf),
            pltpu.VMEM((BLK, nslot * BLK), jnp.float32),
            pltpu.VMEM((heads * BLK, nslot * BLK), bf),
            pltpu.VMEM((heads * BLK, nslot * BLK), bf),
            pltpu.VMEM((heads * BLK, D), bf),
            pltpu.VMEM((heads * BLK, D), bf),
            pltpu.VMEM((half_rows, D), jnp.float32),
            pltpu.VMEM((half_rows, D), jnp.float32),
        ],
        compiler_params=pltpu.CompilerParams(vmem_limit_bytes=48 << 20),
        name="attend",
    )(tab, q, g, kva, kvb)


def per_device(query_rows, key_rows, value_rows, out_grad, block_table, pattern):
    my_x = lax.axis_index("x")
    my_y = lax.axis_index("yh")
    my_core = lax.axis_index("core")
    ctx = my_x * (NY * NC) + my_y * NC + my_core
    held_seq = lax.dynamic_index_in_dim(block_table, ctx, 0, keepdims=False)
    f32 = jnp.float32
    bf = jnp.bfloat16
    own = jnp.concatenate([key_rows, value_rows], axis=0)
    peer = lax.ppermute(own, "yh", SWAP)
    pair = jnp.concatenate([own, peer], axis=0)
    n = pair.shape[0]
    kva = lax.all_to_all(
        jnp.broadcast_to(pair[None], (NX, n, D)), "x", 0, 0, tiled=True
    ).reshape(NX * n, D)
    kvb = lax.ppermute(kva, "core", SWAP)
    tab = slot_tables(block_table, pattern, held_seq, my_y, my_core)
    attended, query_grad, part_a, part_b = attend(
        tab, query_rows, out_grad, kva, kvb, pattern.shape[1]
    )
    other = lax.ppermute(part_b, "core", SWAP)
    both = (part_a.astype(f32) + other.astype(f32)).astype(bf).reshape(NX, n, D)
    from_x = lax.all_to_all(both, "x", 0, 0, tiled=True)
    over_x = jnp.sum(from_x.astype(f32), axis=0)
    from_y = lax.ppermute(over_x[n // 2:].astype(bf), "yh", SWAP)
    total = (over_x[: n // 2] + from_y.astype(f32)).astype(bf)
    return attended, query_grad, total[: n // 4], total[n // 4:]


def solution(mesh):
    dp, head = mesh.shape["dp"], mesh.shape["head"]
    fine = Mesh(mesh.devices.reshape(dp, head, NX, NY, NC), ("dp", "head", "x", "yh", "core"))
    rows = P(("dp", "x", "yh", "core"), "head")
    return jax.shard_map(
        per_device,
        mesh=fine,
        in_specs=(rows, rows, rows, rows, P("dp", None), P("dp", None)),
        out_specs=(rows, rows, rows, rows),
        check_vma=False,
    )
```

time: 323 us -> 101 us (0.31)
  the two profiles are of different devices: /device:TPU:6 before, /device:TPU:16 now
where the time goes in v1:
time: 101 us
  waiting for transfers between devices  34.8 us (34%)
  Pallas kernels  23.5 us (23%)
  blocking collectives  18.1 us (18%)
  starting transfers between devices  17.9 us (18%)
  other arithmetic  3.28 us (3%)
  local copies, waits for them, and re-layouts  2.73 us (3%)
    pallas_call x1, Pallas kernels, attend(): pl.pallas_call(attend_kernel, out_shape=(jax.ShapeDtypeStruct((rows, cols...  23.5 us
    all_to_all x1, blocking collectives, per_device(): from_x = lax.all_to_all(both, 'x', 0, 0, tiled=True)  18.1 us
    all_to_all x1, waiting for transfers between devices, per_device(): lax.all_to_all(jnp.broadcast_to(pair[None], (NX, n, D)), 'x', 0, 0, tiled...  14.6 us
    ppermute x1, waiting for transfers between devices, per_device(): from_y = lax.ppermute(over_x[n // 2:].astype(bf), 'yh', SWAP)  9.96 us
    ppermute x1, waiting for transfers between devices, per_device(): peer = lax.ppermute(own, 'yh', SWAP)  6.56 us
    ppermute x1, starting transfers between devices, per_device(): peer = lax.ppermute(own, 'yh', SWAP)  5.94 us
    all_to_all x1, starting transfers between devices, per_device(): lax.all_to_all(jnp.broadcast_to(pair[None], (NX, n, D)), 'x', 0, 0, tiled...  5.84 us
    ppermute x1, waiting for transfers between devices, per_device(): other = lax.ppermute(part_b, 'core', SWAP)  2.51 us
  transfers between devices with their start and end apart: 5, of which 5 were waited for; matrix products, arithmetic and copies ran while one was open for 2% of the time, Pallas kernels for 0%

profile of v1, /device:TPU:16, one launch (start us, length us, event | category | flops | bytes accessed | tf_op | source)
XLA Modules:
  0.0 101.1 jit_solution(13806524740954715006)
XLA Ops:
  0.6 0.9 pad_maximum_fusion.1
  1.5 5.9 %collective-permute-start = (bf16[512,128]{1,0:T(8,128)(2,1)S(1)}, bf16[512,128]{1,0:T(8,128)(2,1)S(1)}, u32[]{:S(2)}, u32[]{:S(2)}) collective-permute-start(bf16[512,128]{1,0:T(8,128)(2,1)S(1)} %pad_maximum_fusion.1), channel_id=1, source_target_pairs={{0,2},{2,0},{1,3},{3,1},{4,6},{6,4},{5,7},{7,5},{8,10},{10,8},{9,1... | collective-permute-start | bytes 393224 | tf_op jit(solution)/shard_map/ppermute | solution.py:185
  7.5 6.6 %collective-permute-done = bf16[512,128]{1,0:T(8,128)(2,1)S(1)} collective-permute-done((bf16[512,128]{1,0:T(8,128)(2,1)S(1)}, bf16[512,128]{1,0:T(8,128)(2,1)S(1)}, u32[]{:S(2)}, u32[]{:S(2)}) %collective-permute-start) | collective-permute-done | bytes 131104 | tf_op jit(solution)/shard_map/ppermute | solution.py:185
  14.0 0.9 pad_maximum_fusion
  14.9 1.1 %broadcast_in_dim.30 = bf16[4,1024,128]{2,1,0:T(8,128)(2,1)} broadcast(bf16[1024,128]{1,0:T(8,128)(2,1)S(1)} %pad_maximum_fusion), dimensions={1,2} | broadcast | bytes 1310720 | tf_op jit(solution)/shard_map/broadcast_in_dim | solution.py:189
  16.0 5.8 %all-to-all-start = ((bf16[4,1024,128]{2,1,0:T(8,128)(2,1)}), bf16[4,1024,128]{2,1,0:T(8,128)(2,1)S(1)}, u32[]{:S(2)}, u32[]{:S(2)}) async-start(bf16[4,1024,128]{2,1,0:T(8,128)(2,1)} %broadcast_in_dim.30), calls=%async_computation | async-start | bytes 2097152 | tf_op jit(solution)/shard_map/all_to_all | solution.py:188
  21.9 0.2 dynamic-slice_reduce_fusion
  22.2 0.2 multiply_reduce_fusion
  22.5 14.6 %all-to-all-done = bf16[4,1024,128]{2,1,0:T(8,128)(2,1)S(1)} async-done(((bf16[4,1024,128]{2,1,0:T(8,128)(2,1)}), bf16[4,1024,128]{2,1,0:T(8,128)(2,1)S(1)}, u32[]{:S(2)}, u32[]{:S(2)}) %all-to-all-start) | async-done | bytes 1048608 | tf_op jit(solution)/shard_map/all_to_all | solution.py:188
  37.1 1.9 %collective-permute-start.1 = (bf16[4096,128]{1,0:T(8,128)(2,1)S(1)}, bf16[4096,128]{1,0:T(8,128)(2,1)S(1)}, u32[]{:S(2)}, u32[]{:S(2)}) collective-permute-start(bf16[4096,128]{1,0:T(8,128)(2,1)S(1)} %bitcast.2), channel_id=1, source_target_pairs={{0,1},{1,0},{2,3},{3,2},{4,5},{5,4},{6,7},{7,6},{8,9},{9,8},{10,11... | collective-permute-start | bytes 3145736 | tf_op jit(solution)/shard_map/ppermute | solution.py:191
  39.0 0.2 and_reduce_fusion
  39.2 0.1 copy.18
  39.4 0.1 copy.19
  39.7 0.3 fusion.1
  40.4 1.2 %collective-permute-done.1.kvb_ref = bf16[4096,128]{1,0:T(8,128)(2,1)S(1)} collective-permute-done((bf16[4096,128]{1,0:T(8,128)(2,1)S(1)}, bf16[4096,128]{1,0:T(8,128)(2,1)S(1)}, u32[]{:S(2)}, u32[]{:S(2)}) %collective-permute-start.1) | collective-permute-done | bytes 1048608 | tf_op jit(solution)/shard_map/ppermute | solution.py:191
  41.6 23.5 %attend.1 = (bf16[256,1024]{1,0:T(8,128)(2,1)}, bf16[256,1024]{1,0:T(8,128)(2,1)}, bf16[4096,128]{1,0:T(8,128)(2,1)S(1)}, bf16[4096,128]{1,0:T(8,128)(2,1)S(1)}) custom-call(s32[60]{0:T(128)S(1)} %pad_add_fusion.tab, bf16[256,1024]{1,0:T(8,128)(2,1)S(1)} %copy-done, bf16[256,1024]{1,0:T(8,128)(2,1)S(1)} %copy-done.1, bf16[4096,128]{1,0:T(8,128)(2,1)S(1)} %bitcast.3, ...), custom_call_target="tpu_custom_call" | custom-call | tf_op jit(solution)/shard_map/attend/pallas_call | solution.py:150
  65.1 2.0 %collective-permute-start.2 = (bf16[4096,128]{1,0:T(8,128)(2,1)S(1)}, bf16[4096,128]{1,0:T(8,128)(2,1)S(1)}, u32[]{:S(2)}, u32[]{:S(2)}) collective-permute-start(bf16[4096,128]{1,0:T(8,128)(2,1)S(1)} %get-tuple-element.11), channel_id=1, source_target_pairs={{0,1},{1,0},{2,3},{3,2},{4,5},{5,4},{6,7},{7,6},{8,9},{9,8},{10,11... | collective-permute-start | bytes 3145736 | tf_op jit(solution)/shard_map/ppermute | solution.py:196
  67.2 2.5 %collective-permute-done.2 = bf16[4096,128]{1,0:T(8,128)(2,1)S(1)} collective-permute-done((bf16[4096,128]{1,0:T(8,128)(2,1)S(1)}, bf16[4096,128]{1,0:T(8,128)(2,1)S(1)}, u32[]{:S(2)}, u32[]{:S(2)}) %collective-permute-start.2) | collective-permute-done | bytes 1048608 | tf_op jit(solution)/shard_map/ppermute | solution.py:196
  69.7 0.3 add_convert_fusion
  70.0 18.1 %all_to_all.10 = bf16[4,1024,128]{2,1,0:T(8,128)(2,1)S(1)} all-to-all(bf16[4,1024,128]{2,1,0:T(8,128)(2,1)S(1)} %bitcast.4), channel_id=1, replica_groups=mesh['dp'=4,'head'=8,'x'=4,'yh'=2,'core'=2] {'x'}, dimensions={0} | all-to-all | bytes 2097152 | tf_op jit(solution)/shard_map/all_to_all | solution.py:198
  88.1 0.1 convert_reduce_fusion
  88.2 2.2 %collective-permute-start.3 = (bf16[512,128]{1,0:T(8,128)(2,1)S(1)}, bf16[512,128]{1,0:T(8,128)(2,1)S(1)}, u32[]{:S(2)}, u32[]{:S(2)}) collective-permute-start(bf16[512,128]{1,0:T(8,128)(2,1)S(1)} %slice.25), channel_id=1, source_target_pairs={{0,2},{2,0},{1,3},{3,1},{4,6},{6,4},{5,7},{7,5},{8,10},{10,8},{9,1... | collective-permute-start | bytes 393224 | tf_op jit(solution)/shard_map/ppermute | solution.py:200
  90.4 10.0 %collective-permute-done.3 = bf16[512,128]{1,0:T(8,128)(2,1)S(1)} collective-permute-done((bf16[512,128]{1,0:T(8,128)(2,1)S(1)}, bf16[512,128]{1,0:T(8,128)(2,1)S(1)}, u32[]{:S(2)}, u32[]{:S(2)}) %collective-permute-start.3) | collective-permute-done | bytes 131104 | tf_op jit(solution)/shard_map/ppermute | solution.py:200
  100.4 0.7 fusion.9
  (23 shorter events, 0.9 us)
Async XLA Ops:
  1.5 12.5 %collective-permute-start = (bf16[512,128]{1,0:T(8,128)(2,1)S(1)}, bf16[512,128]{1,0:T(8,128)(2,1)S(1)}, u32[]{:S(2)}, u32[]{:S(2)}) collective-permute-start(bf16[512,128]{1,0:T(8,128)(2,1)S(1)} %pad_maximum_fusion.1), channel_id=1, source_target_pairs={{0,2},{2,0},{1,3},{3,1},{4,6},{6,4},{5,7},{7,5},{8,10},{10,8},{9,1... | collective-permute-start | bytes 393224 | tf_op jit(solution)/shard_map/ppermute | solution.py:185
  16.0 5.9 %copy-start.3 = (s32[16,2]{0,1:T(2,128)S(1)}, s32[16,2]{0,1:T(2,128)}, u32[]{:S(2)}) copy-start(s32[16,2]{0,1:T(2,128)} %param.10) | copy-start | bytes 388
  16.0 6.1 %copy-start.2 = (s32[32,10]{0,1:T(8,128)S(1)}, s32[32,10]{0,1:T(8,128)}, u32[]{:S(2)}) copy-start(s32[32,10]{0,1:T(8,128)} %param.11) | copy-start | bytes 3844
  16.0 25.6 %copy-start = (bf16[256,1024]{1,0:T(8,128)(2,1)S(1)}, bf16[256,1024]{1,0:T(8,128)(2,1)}, u32[]{:S(2)}) copy-start(bf16[256,1024]{1,0:T(8,128)(2,1)} %q_ref.1) | copy-start | bytes 1572868
  16.0 25.6 %copy-start.1 = (bf16[256,1024]{1,0:T(8,128)(2,1)S(1)}, bf16[256,1024]{1,0:T(8,128)(2,1)}, u32[]{:S(2)}) copy-start(bf16[256,1024]{1,0:T(8,128)(2,1)} %g_ref.1) | copy-start | bytes 1572868
  16.0 21.0 %all-to-all-start = ((bf16[4,1024,128]{2,1,0:T(8,128)(2,1)}), bf16[4,1024,128]{2,1,0:T(8,128)(2,1)S(1)}, u32[]{:S(2)}, u32[]{:S(2)}) async-start(bf16[4,1024,128]{2,1,0:T(8,128)(2,1)} %broadcast_in_dim.30), calls=%async_computation | async-start | bytes 2097152 | tf_op jit(solution)/shard_map/all_to_all | solution.py:188
  37.1 4.5 %collective-permute-start.1 = (bf16[4096,128]{1,0:T(8,128)(2,1)S(1)}, bf16[4096,128]{1,0:T(8,128)(2,1)S(1)}, u32[]{:S(2)}, u32[]{:S(2)}) collective-permute-start(bf16[4096,128]{1,0:T(8,128)(2,1)S(1)} %bitcast.2), channel_id=1, source_target_pairs={{0,1},{1,0},{2,3},{3,2},{4,5},{5,4},{6,7},{7,6},{8,9},{9,8},{10,11... | collective-permute-start | bytes 3145736 | tf_op jit(solution)/shard_map/ppermute | solution.py:191
  65.1 4.5 %collective-permute-start.2 = (bf16[4096,128]{1,0:T(8,128)(2,1)S(1)}, bf16[4096,128]{1,0:T(8,128)(2,1)S(1)}, u32[]{:S(2)}, u32[]{:S(2)}) collective-permute-start(bf16[4096,128]{1,0:T(8,128)(2,1)S(1)} %get-tuple-element.11), channel_id=1, source_target_pairs={{0,1},{1,0},{2,3},{3,2},{4,5},{5,4},{6,7},{7,6},{8,9},{9,8},{10,11... | collective-permute-start | bytes 3145736 | tf_op jit(solution)/shard_map/ppermute | solution.py:196
  88.2 12.1 %collective-permute-start.3 = (bf16[512,128]{1,0:T(8,128)(2,1)S(1)}, bf16[512,128]{1,0:T(8,128)(2,1)S(1)}, u32[]{:S(2)}, u32[]{:S(2)}) collective-permute-start(bf16[512,128]{1,0:T(8,128)(2,1)S(1)} %slice.25), channel_id=1, source_target_pairs={{0,2},{2,0},{1,3},{3,1},{4,6},{6,4},{5,7},{7,5},{8,10},{10,8},{9,1... | collective-permute-start | bytes 393224 | tf_op jit(solution)/shard_map/ppermute | solution.py:200

commit v2 on v1

v2 whole, which is shorter than its diff:
```python
import math

import jax
import jax.numpy as jnp
from jax import lax
from jax.experimental import pallas as pl
from jax.experimental.pallas import tpu as pltpu
from jax.sharding import Mesh, PartitionSpec as P

D = 128
BLK = 128
NX, NY, NC = 4, 2, 2
NEG = -1e30
RC = 16
VMEM_PARTS = 28
VMEM_ROWS = 16
SWAP = [(0, 1), (1, 0)]


def slot_tables(block_table, pattern, held_seq, my_y, my_core):
    blocks = pattern.shape[0]
    slots = pattern.shape[1]
    block_ids = jnp.arange(blocks, dtype=jnp.int32)
    store_seq = block_table.reshape(-1)
    inverse = jnp.sum(
        jnp.where(store_seq[:, None] == block_ids[None, :], block_ids[:, None], 0), axis=0
    )
    onehot = (held_seq[:, None] == block_ids[None, :]).astype(jnp.int32)
    held_pattern = jnp.sum(onehot[:, :, None] * pattern[None, :, :], axis=1)
    store = jnp.sum(
        jnp.where(held_pattern[:, :, None] == block_ids[None, None, :], inverse[None, None, :], 0),
        axis=2,
    )
    same = held_pattern[:, :, None] == held_pattern[:, None, :]
    slot_ids = jnp.arange(slots, dtype=jnp.int32)
    before = slot_ids[None, :] < slot_ids[:, None]
    live = jnp.logical_not(jnp.any(same & before[None], axis=2)).astype(jnp.int32)
    diag = (held_pattern == held_seq[:, None]).astype(jnp.int32)
    sub = store % 2
    dev = store // 2
    core = dev % 2
    yh = (dev // 2) % 2
    xi = dev // 4
    half = jnp.bitwise_xor(core, my_core)
    row = xi * 1024 + yh * 512 + sub * BLK
    part_row = xi * 1024 + jnp.bitwise_xor(yh, my_y) * 512 + sub * BLK
    kind = live * (1 + diag)
    tables = [half, row, kind, part_row]
    return jnp.concatenate([t.reshape(-1) for t in tables]).astype(jnp.int32)


def load_keys(b, nslot, ns, tab, kva_ref, kvb_ref, kg, vg):
    for j in range(nslot):
        t = b * nslot + j
        half = tab[t]
        row = pl.multiple_of(tab[ns + t], BLK)
        dst = pl.ds(j * BLK, BLK)

        @pl.when(half == 0)
        def _():
            kg[dst, :] = kva_ref[pl.ds(row, BLK), :]
            vg[dst, :] = kva_ref[pl.ds(row + 256, BLK), :]

        @pl.when(half == 1)
        def _():
            kg[dst, :] = kvb_ref[pl.ds(row, BLK), :]
            vg[dst, :] = kvb_ref[pl.ds(row + 256, BLK), :]


def part_kernel(
    tab, q_ref, g_ref, kva_ref, kvb_ref, pa_ref, pb_ref, p_ref, ds_ref,
    kg, vg, bias, qs, gs, s_sc, gp_sc, p_sc, ds_sc, acc_a, acc_b,
):
    nslot = kg.shape[0] // BLK
    per = q_ref.shape[0] // BLK
    ns = per * nslot
    heads = q_ref.shape[1] // D
    stacked = heads * BLK
    scale = D ** -0.5
    c2 = scale * math.log2(math.e)
    nt = (((1,), (1,)), ((), ()))
    tn = (((0,), (0,)), ((), ()))
    acc_a[...] = jnp.zeros_like(acc_a)
    acc_b[...] = jnp.zeros_like(acc_b)

    def one_block(b, _):
        r0 = pl.multiple_of(b * BLK, BLK)
        s0 = pl.multiple_of(b * stacked, stacked)
        load_keys(b, nslot, ns, tab, kva_ref, kvb_ref, kg, vg)
        for j in range(nslot):
            kind = tab[2 * ns + b * nslot + j]
            ri = lax.broadcasted_iota(jnp.int32, (BLK, BLK), 0)
            ci = lax.broadcasted_iota(jnp.int32, (BLK, BLK), 1)
            ok = jnp.logical_or(ci <= ri, kind != 2)
            ok = jnp.logical_and(ok, kind > 0)
            bias[:, j * BLK:(j + 1) * BLK] = jnp.where(ok, 0.0, NEG)
        for h in range(heads):
            qs[h * BLK:(h + 1) * BLK, :] = q_ref[pl.ds(r0, BLK), h * D:(h + 1) * D]
            gs[h * BLK:(h + 1) * BLK, :] = g_ref[pl.ds(r0, BLK), h * D:(h + 1) * D]
        s_sc[...] = lax.dot_general(qs[...], kg[...], nt, preferred_element_type=jnp.float32)
        gp_sc[...] = lax.dot_general(gs[...], vg[...], nt, preferred_element_type=jnp.float32)
        for r in range(0, stacked, RC):
            rr = slice(r, r + RC)
            out = pl.ds(s0 + r, RC)
            s = s_sc[rr, :] * c2 + bias[r % BLK:r % BLK + RC, :]
            m = jnp.max(s, axis=1, keepdims=True)
            e = jnp.exp2(s - m)
            prob = e * (1.0 / jnp.sum(e, axis=1, keepdims=True))
            p_sc[rr, :] = prob.astype(jnp.bfloat16)
            gp = gp_sc[rr, :]
            rd = jnp.sum(prob * gp, axis=1, keepdims=True)
            ds_sc[rr, :] = (prob * (gp - rd)).astype(jnp.bfloat16)
        mine = pl.ds(s0, stacked)
        p_ref[mine, :] = p_sc[...]
        ds_ref[mine, :] = ds_sc[...]
        dk_all = lax.dot_general(ds_sc[...], qs[...], tn, preferred_element_type=jnp.float32) * scale
        dv_all = lax.dot_general(p_sc[...], gs[...], tn, preferred_element_type=jnp.float32)
        for j in range(nslot):
            t = b * nslot + j
            half = tab[t]
            row = pl.multiple_of(tab[3 * ns + t], BLK)
            rows_k = pl.ds(row, BLK)
            rows_v = pl.ds(row + 256, BLK)
            dk_j = dk_all[j * BLK:(j + 1) * BLK]
            dv_j = dv_all[j * BLK:(j + 1) * BLK]

            @pl.when(half == 0)
            def _():
                acc_a[rows_k, :] += dk_j
                acc_a[rows_v, :] += dv_j

            @pl.when(half == 1)
            def _():
                acc_b[rows_k, :] += dk_j
                acc_b[rows_v, :] += dv_j
        return 0

    lax.fori_loop(0, per, one_block, 0)
    pa_ref[...] = acc_a[...].astype(jnp.bfloat16)
    pb_ref[...] = acc_b[...].astype(jnp.bfloat16)


def row_kernel(tab, p_ref, ds_ref, kva_ref, kvb_ref, att_ref, qg_ref, kg, vg):
    nslot = kg.shape[0] // BLK
    per = att_ref.shape[0] // BLK
    heads = att_ref.shape[1] // D
    stacked = heads * BLK
    scale = D ** -0.5

    def one_block(b, _):
        load_keys(b, nslot, per * nslot, tab, kva_ref, kvb_ref, kg, vg)
        r0 = pl.multiple_of(b * BLK, BLK)
        mine = pl.ds(pl.multiple_of(b * stacked, stacked), stacked)
        wide = jnp.dot(p_ref[mine, :], vg[...], preferred_element_type=jnp.float32)
        qg = jnp.dot(ds_ref[mine, :], kg[...], preferred_element_type=jnp.float32) * scale
        for h in range(heads):
            cols = slice(h * D, (h + 1) * D)
            hr = slice(h * BLK, (h + 1) * BLK)
            att_ref[pl.ds(r0, BLK), cols] = wide[hr].astype(jnp.bfloat16)
            qg_ref[pl.ds(r0, BLK), cols] = qg[hr].astype(jnp.bfloat16)
        return 0

    lax.fori_loop(0, per, one_block, 0)


VM = pl.BlockSpec(memory_space=pltpu.VMEM)
SM = pl.BlockSpec(memory_space=pltpu.SMEM)


def parts(tab, q, g, kva, kvb, nslot):
    per = q.shape[0] // BLK
    stacked = q.shape[1] // D * BLK
    bf, f32 = jnp.bfloat16, jnp.float32
    keys = nslot * BLK
    shapes = (kva.shape, kvb.shape, (per * stacked, keys), (per * stacked, keys))
    work = per * stacked * keys
    return pl.pallas_call(
        part_kernel,
        out_shape=tuple(jax.ShapeDtypeStruct(s, bf) for s in shapes),
        in_specs=[SM, VM, VM, VM, VM],
        out_specs=(VM, VM, VM, VM),
        scratch_shapes=[
            pltpu.VMEM((keys, D), bf),
            pltpu.VMEM((keys, D), bf),
            pltpu.VMEM((BLK, keys), f32),
            pltpu.VMEM((stacked, D), bf),
            pltpu.VMEM((stacked, D), bf),
            pltpu.VMEM((stacked, keys), f32),
            pltpu.VMEM((stacked, keys), f32),
            pltpu.VMEM((stacked, keys), bf),
            pltpu.VMEM((stacked, keys), bf),
            pltpu.VMEM(kva.shape, f32),
            pltpu.VMEM(kvb.shape, f32),
        ],
        compiler_params=pltpu.CompilerParams(vmem_limit_bytes=VMEM_PARTS << 20),
        cost_estimate=pl.CostEstimate(
            flops=8 * D * work, transcendentals=work, bytes_accessed=6 << 20
        ),
        name="parts",
    )(tab, q, g, kva, kvb)


def rows(tab, p, ds, kva, kvb, shape, nslot):
    bf = jnp.bfloat16
    keys = nslot * BLK
    return pl.pallas_call(
        row_kernel,
        out_shape=tuple(jax.ShapeDtypeStruct(shape, bf) for _ in range(2)),
        in_specs=[SM, VM, VM, VM, VM],
        out_specs=(VM, VM),
        scratch_shapes=[pltpu.VMEM((keys, D), bf), pltpu.VMEM((keys, D), bf)],
        compiler_params=pltpu.CompilerParams(vmem_limit_bytes=VMEM_ROWS << 20),
        cost_estimate=pl.CostEstimate(
            flops=4 * D * p.shape[0] * keys, transcendentals=0, bytes_accessed=6 << 20
        ),
        name="rows",
    )(tab, p, ds, kva, kvb)


def per_device(query_rows, key_rows, value_rows, out_grad, block_table, pattern):
    my_x = lax.axis_index("x")
    my_y = lax.axis_index("yh")
    my_core = lax.axis_index("core")
    ctx = my_x * (NY * NC) + my_y * NC + my_core
    held_seq = lax.dynamic_index_in_dim(block_table, ctx, 0, keepdims=False)
    f32 = jnp.float32
    bf = jnp.bfloat16
    own = jnp.concatenate([key_rows, value_rows], axis=0)
    pair = lax.all_gather(own, "yh", axis=0, tiled=True)
    n = pair.shape[0]
    kva = lax.all_to_all(
        jnp.broadcast_to(pair[None], (NX, n, D)), "x", 0, 0, tiled=True
    ).reshape(NX * n, D)
    kvb = lax.ppermute(kva, "core", SWAP)
    tab = slot_tables(block_table, pattern, held_seq, my_y, my_core)
    nslot = pattern.shape[1]
    part_a, part_b, prob, grad_score = parts(tab, query_rows, out_grad, kva, kvb, nslot)
    other = lax.ppermute(part_b, "core", SWAP)
    both = (part_a.astype(f32) + other.astype(f32)).astype(bf).reshape(NX, n, D)
    both, prob, grad_score = lax.optimization_barrier((both, prob, grad_score))
    attended, query_grad = rows(tab, prob, grad_score, kva, kvb, query_rows.shape, nslot)
    from_x = lax.all_to_all(both, "x", 0, 0, tiled=True)
    over_x = jnp.sum(from_x.astype(f32), axis=0)
    from_y = lax.ppermute(over_x[n // 2:].astype(bf), "yh", SWAP)
    total = (over_x[: n // 2] + from_y.astype(f32)).astype(bf)
    return attended, query_grad, total[: n // 4], total[n // 4:]


def solution(mesh):
    dp, head = mesh.shape["dp"], mesh.shape["head"]
    fine = Mesh(mesh.devices.reshape(dp, head, NX, NY, NC), ("dp", "head", "x", "yh", "core"))
    spec = P(("dp", "x", "yh", "core"), "head")
    return jax.shard_map(
        per_device,
        mesh=fine,
        in_specs=(spec, spec, spec, spec, P("dp", None), P("dp", None)),
        out_specs=(spec, spec, spec, spec),
        check_vma=False,
    )
```

time: 101 us -> 86.6 us (0.86)
  waiting for transfers between devices: 34.8 us -> 23.4 us
  blocking collectives: 18.1 us -> 29.4 us
  Pallas kernels: 23.5 us -> 15.7 us
  starting transfers between devices: 17.9 us -> 11.8 us
    all_gather x0 -> x1, blocking collectives: none -> 11.3 us  [per_device(): pair = lax.all_gather(own, 'yh', axis=0, tiled=True)]
    pallas_call x1 -> x2, Pallas kernels: 23.5 us -> 15.7 us  [the longest x1 10.9 us: parts(): pl.pallas_call(part_kernel, out_shape=tuple((jax.ShapeDtypeStruct(s, bf)...]
    ppermute x1 -> x0, waiting for transfers between devices: 6.56 us -> none  [per_device(): peer = lax.ppermute(own, 'yh', SWAP)]
    ppermute x1 -> x0, starting transfers between devices: 5.94 us -> none  [per_device(): peer = lax.ppermute(own, 'yh', SWAP)]
    ppermute x1, waiting for transfers between devices: 9.96 us -> 5.12 us  [per_device(): from_y = lax.ppermute(over_x[n // 2:].astype(bf), 'yh', SWAP)]
  transfers between devices with their start and end apart: 5 -> 4, of which waited for: 5 -> 4; matrix products, arithmetic and copies ran while one was open for 2% -> 2% of each run, Pallas kernels for 0% -> 6%
where the time goes in v2:
time: 86.6 us; the launch traced here: 86.3 us
  blocking collectives  29.4 us (34%)
  waiting for transfers between devices  23.4 us (27%)
  Pallas kernels  15.7 us (18%)
  starting transfers between devices  11.8 us (14%)
  local copies, waits for them, and re-layouts  2.72 us (3%)
  other arithmetic  2.48 us (3%)
    all_to_all x1, blocking collectives, per_device(): from_x = lax.all_to_all(both, 'x', 0, 0, tiled=True)  18.1 us
    all_to_all x1, waiting for transfers between devices, per_device(): lax.all_to_all(jnp.broadcast_to(pair[None], (NX, n, D)), 'x', 0, 0, tiled...  14.3 us
    all_gather x1, blocking collectives, per_device(): pair = lax.all_gather(own, 'yh', axis=0, tiled=True)  11.3 us
    pallas_call x1, Pallas kernels, parts(): pl.pallas_call(part_kernel, out_shape=tuple((jax.ShapeDtypeStruct(s, bf)...  10.9 us
    all_to_all x1, starting transfers between devices, per_device(): lax.all_to_all(jnp.broadcast_to(pair[None], (NX, n, D)), 'x', 0, 0, tiled...  5.7 us
    ppermute x1, waiting for transfers between devices, per_device(): from_y = lax.ppermute(over_x[n // 2:].astype(bf), 'yh', SWAP)  5.12 us
    pallas_call x1, Pallas kernels, rows(): pl.pallas_call(row_kernel, out_shape=tuple((jax.ShapeDtypeStruct(shape, b...  4.86 us
    ppermute x1, waiting for transfers between devices, per_device(): other = lax.ppermute(part_b, 'core', SWAP)  2.5 us
  transfers between devices with their start and end apart: 4, of which 4 were waited for; matrix products, arithmetic and copies ran while one was open for 2% of the time, Pallas kernels for 6%

profile of v2, /device:TPU:16, one launch (start us, length us, event | category | flops | bytes accessed | tf_op | source)
XLA Modules:
  0.0 86.3 jit_solution(7393090992084940412)
XLA Ops:
  0.7 1.0 %pad_maximum_fusion = bf16[512,128]{1,0:T(8,128)(2,1)S(1)} fusion(bf16[256,128]{1,0:T(8,128)(2,1)} %param.8, bf16[256,128]{1,0:T(8,128)(2,1)} %param.7), kind=kLoop, calls=%fused_computation.5 | loop fusion | flops 262144 | bytes 262144 | tf_op jit(solution)/shard_map/concatenate | solution.py:228
  1.6 11.3 %all_gather.3 = bf16[1024,128]{1,0:T(8,128)(2,1)S(1)} all-gather(bf16[512,128]{1,0:T(8,128)(2,1)S(1)} %pad_maximum_fusion), channel_id=1, replica_groups=mesh['dp'=4,'head'=8,'x'=4,'yh'=2,'core'=2] {'yh'}, dimensions={0}, use_global_device_ids=true | all-gather | bytes 393216 | tf_op jit(solution)/shard_map/all_gather | solution.py:229
  12.9 1.1 %broadcast_in_dim.30 = bf16[4,1024,128]{2,1,0:T(8,128)(2,1)} broadcast(bf16[1024,128]{1,0:T(8,128)(2,1)S(1)} %all_gather.3), dimensions={1,2} | broadcast | bytes 1310720 | tf_op jit(solution)/shard_map/broadcast_in_dim | solution.py:232
  14.0 5.7 %all-to-all-start = ((bf16[4,1024,128]{2,1,0:T(8,128)(2,1)}), bf16[4,1024,128]{2,1,0:T(8,128)(2,1)S(1)}, u32[]{:S(2)}, u32[]{:S(2)}) async-start(bf16[4,1024,128]{2,1,0:T(8,128)(2,1)} %broadcast_in_dim.30), calls=%async_computation | async-start | bytes 2097152 | tf_op jit(solution)/shard_map/all_to_all | solution.py:231
  19.7 0.2 dynamic-slice_reduce_fusion
  20.0 0.2 multiply_reduce_fusion
  20.2 0.1 copy.16
  20.3 0.2 and_reduce_fusion
  20.5 0.1 copy.18
  20.6 14.3 %all-to-all-done = bf16[4,1024,128]{2,1,0:T(8,128)(2,1)S(1)} async-done(((bf16[4,1024,128]{2,1,0:T(8,128)(2,1)}), bf16[4,1024,128]{2,1,0:T(8,128)(2,1)S(1)}, u32[]{:S(2)}, u32[]{:S(2)}) %all-to-all-start) | async-done | bytes 1048608 | tf_op jit(solution)/shard_map/all_to_all | solution.py:231
  34.9 1.9 %collective-permute-start = (bf16[4096,128]{1,0:T(8,128)(2,1)S(1)}, bf16[4096,128]{1,0:T(8,128)(2,1)S(1)}, u32[]{:S(2)}, u32[]{:S(2)}) collective-permute-start(bf16[4096,128]{1,0:T(8,128)(2,1)S(1)} %bitcast.2), channel_id=1, source_target_pairs={{0,1},{1,0},{2,3},{3,2},{4,5},{5,4},{6,7},{7,6},{8,9},{9,8},{10,11... | collective-permute-start | bytes 3145736 | tf_op jit(solution)/shard_map/ppermute | solution.py:234
  37.3 0.3 fusion.1
  37.6 0.1 copy.15
  37.9 1.5 %collective-permute-done.kvb_ref = bf16[4096,128]{1,0:T(8,128)(2,1)S(1)} collective-permute-done((bf16[4096,128]{1,0:T(8,128)(2,1)S(1)}, bf16[4096,128]{1,0:T(8,128)(2,1)S(1)}, u32[]{:S(2)}, u32[]{:S(2)}) %collective-permute-start) | collective-permute-done | bytes 1048608 | tf_op jit(solution)/shard_map/ppermute | solution.py:234
  39.4 10.9 %parts.1 = (bf16[4096,128]{1,0:T(8,128)(2,1)S(1)}, bf16[4096,128]{1,0:T(8,128)(2,1)S(1)}, bf16[2048,1280]{1,0:T(8,128)(2,1)S(1)}, bf16[2048,1280]{1,0:T(8,128)(2,1)S(1)}) custom-call(s32[80]{0:T(128)S(1)} %pad_add_fusion.tab, bf16[256,1024]{1,0:T(8,128)(2,1)S(1)} %copy-done, bf16[256,1024]{1,0:T(8,128)(2,1)S(1)} %copy-done.1, bf16[4096,128]{1,0:T(8,128)(2,1)S(1)} %bitcast.3, ...), custom_call_target="tpu_custom_call" | custom-call | flops 2684354560 | bytes 6291456 | tf_op jit(solution)/shard_map/parts/pallas_call | solution.py:177
  50.3 2.0 %collective-permute-start.1 = (bf16[4096,128]{1,0:T(8,128)(2,1)S(1)}, bf16[4096,128]{1,0:T(8,128)(2,1)S(1)}, u32[]{:S(2)}, u32[]{:S(2)}) collective-permute-start(bf16[4096,128]{1,0:T(8,128)(2,1)S(1)} %get-tuple-element.14), channel_id=1, source_target_pairs={{0,1},{1,0},{2,3},{3,2},{4,5},{5,4},{6,7},{7,6},{8,9},{9,8},{10,11... | collective-permute-start | bytes 3145736 | tf_op jit(solution)/shard_map/ppermute | solution.py:238
  52.4 2.5 %collective-permute-done.1 = bf16[4096,128]{1,0:T(8,128)(2,1)S(1)} collective-permute-done((bf16[4096,128]{1,0:T(8,128)(2,1)S(1)}, bf16[4096,128]{1,0:T(8,128)(2,1)S(1)}, u32[]{:S(2)}, u32[]{:S(2)}) %collective-permute-start.1) | collective-permute-done | bytes 1048608 | tf_op jit(solution)/shard_map/ppermute | solution.py:238
  54.9 0.3 add_convert_fusion
  55.1 18.1 %all_to_all.10 = bf16[4,1024,128]{2,1,0:T(8,128)(2,1)S(1)} all-to-all(bf16[4,1024,128]{2,1,0:T(8,128)(2,1)S(1)} %bitcast.5), channel_id=1, replica_groups=mesh['dp'=4,'head'=8,'x'=4,'yh'=2,'core'=2] {'x'}, dimensions={0} | all-to-all | bytes 2097152 | tf_op jit(solution)/shard_map/all_to_all | solution.py:242
  73.2 0.1 convert_reduce_fusion
  73.4 2.2 %collective-permute-start.2 = (bf16[512,128]{1,0:T(8,128)(2,1)S(1)}, bf16[512,128]{1,0:T(8,128)(2,1)S(1)}, u32[]{:S(2)}, u32[]{:S(2)}) collective-permute-start(bf16[512,128]{1,0:T(8,128)(2,1)S(1)} %slice.25), channel_id=1, source_target_pairs={{0,2},{2,0},{1,3},{3,1},{4,6},{6,4},{5,7},{7,5},{8,10},{10,8},{9,1... | collective-permute-start | bytes 393224 | tf_op jit(solution)/shard_map/ppermute | solution.py:244
  75.6 4.9 %rows.1 = (bf16[256,1024]{1,0:T(8,128)(2,1)}, bf16[256,1024]{1,0:T(8,128)(2,1)}) custom-call(s32[80]{0:T(128)S(1)} %pad_add_fusion.tab, bf16[2048,1280]{1,0:T(8,128)(2,1)S(1)} %get-tuple-element.17.p_ref, bf16[2048,1280]{1,0:T(8,128)(2,1)S(1)} %get-tuple-element.18.ds_ref, bf16[4096,128]{1,0:T(8,128)(2,1)S(1)} %bitcast.4, ...), custom_call_target="tpu_custom_call" | custom-call | flops 1342177280 | bytes 6291456 | tf_op jit(solution)/shard_map/rows/pallas_call | solution.py:206
  80.4 5.1 %collective-permute-done.2 = bf16[512,128]{1,0:T(8,128)(2,1)S(1)} collective-permute-done((bf16[512,128]{1,0:T(8,128)(2,1)S(1)}, bf16[512,128]{1,0:T(8,128)(2,1)S(1)}, u32[]{:S(2)}, u32[]{:S(2)}) %collective-permute-start.2) | collective-permute-done | bytes 131104 | tf_op jit(solution)/shard_map/ppermute | solution.py:244
  85.6 0.7 fusion.8
  (23 shorter events, 0.8 us)
Async XLA Ops:
  0.6 19.1 %copy-start.3 = (s32[16,2]{0,1:T(2,128)S(1)}, s32[16,2]{0,1:T(2,128)}, u32[]{:S(2)}) copy-start(s32[16,2]{0,1:T(2,128)} %param.10) | copy-start | bytes 388
  0.6 19.3 %copy-start.2 = (s32[32,10]{0,1:T(8,128)S(1)}, s32[32,10]{0,1:T(8,128)}, u32[]{:S(2)}) copy-start(s32[32,10]{0,1:T(8,128)} %param.11) | copy-start | bytes 3844
  0.7 38.8 %copy-start.1 = (bf16[256,1024]{1,0:T(8,128)(2,1)S(1)}, bf16[256,1024]{1,0:T(8,128)(2,1)}, u32[]{:S(2)}) copy-start(bf16[256,1024]{1,0:T(8,128)(2,1)} %g_ref.1) | copy-start | bytes 1572868
  0.7 38.8 %copy-start = (bf16[256,1024]{1,0:T(8,128)(2,1)S(1)}, bf16[256,1024]{1,0:T(8,128)(2,1)}, u32[]{:S(2)}) copy-start(bf16[256,1024]{1,0:T(8,128)(2,1)} %q_ref.1) | copy-start | bytes 1572868
  14.0 20.9 %all-to-all-start = ((bf16[4,1024,128]{2,1,0:T(8,128)(2,1)}), bf16[4,1024,128]{2,1,0:T(8,128)(2,1)S(1)}, u32[]{:S(2)}, u32[]{:S(2)}) async-start(bf16[4,1024,128]{2,1,0:T(8,128)(2,1)} %broadcast_in_dim.30), calls=%async_computation | async-start | bytes 2097152 | tf_op jit(solution)/shard_map/all_to_all | solution.py:231
  34.9 4.5 %collective-permute-start = (bf16[4096,128]{1,0:T(8,128)(2,1)S(1)}, bf16[4096,128]{1,0:T(8,128)(2,1)S(1)}, u32[]{:S(2)}, u32[]{:S(2)}) collective-permute-start(bf16[4096,128]{1,0:T(8,128)(2,1)S(1)} %bitcast.2), channel_id=1, source_target_pairs={{0,1},{1,0},{2,3},{3,2},{4,5},{5,4},{6,7},{7,6},{8,9},{9,8},{10,11... | collective-permute-start | bytes 3145736 | tf_op jit(solution)/shard_map/ppermute | solution.py:234
  50.3 4.6 %collective-permute-start.1 = (bf16[4096,128]{1,0:T(8,128)(2,1)S(1)}, bf16[4096,128]{1,0:T(8,128)(2,1)S(1)}, u32[]{:S(2)}, u32[]{:S(2)}) collective-permute-start(bf16[4096,128]{1,0:T(8,128)(2,1)S(1)} %get-tuple-element.14), channel_id=1, source_target_pairs={{0,1},{1,0},{2,3},{3,2},{4,5},{5,4},{6,7},{7,6},{8,9},{9,8},{10,11... | collective-permute-start | bytes 3145736 | tf_op jit(solution)/shard_map/ppermute | solution.py:238
  73.4 12.1 %collective-permute-start.2 = (bf16[512,128]{1,0:T(8,128)(2,1)S(1)}, bf16[512,128]{1,0:T(8,128)(2,1)S(1)}, u32[]{:S(2)}, u32[]{:S(2)}) collective-permute-start(bf16[512,128]{1,0:T(8,128)(2,1)S(1)} %slice.25), channel_id=1, source_target_pairs={{0,2},{2,0},{1,3},{3,1},{4,6},{6,4},{5,7},{7,5},{8,10},{10,8},{9,1... | collective-permute-start | bytes 393224 | tf_op jit(solution)/shard_map/ppermute | solution.py:244

commit v3 on v2

--- a/solution.py
+++ b/solution.py
@@ -17,36 +17,32 @@
 SWAP = [(0, 1), (1, 0)]
 
 
-def slot_tables(block_table, pattern, held_seq, my_y, my_core):
-    blocks = pattern.shape[0]
-    slots = pattern.shape[1]
-    block_ids = jnp.arange(blocks, dtype=jnp.int32)
-    store_seq = block_table.reshape(-1)
-    inverse = jnp.sum(
-        jnp.where(store_seq[:, None] == block_ids[None, :], block_ids[:, None], 0), axis=0
-    )
-    onehot = (held_seq[:, None] == block_ids[None, :]).astype(jnp.int32)
-    held_pattern = jnp.sum(onehot[:, :, None] * pattern[None, :, :], axis=1)
-    store = jnp.sum(
-        jnp.where(held_pattern[:, :, None] == block_ids[None, None, :], inverse[None, None, :], 0),
-        axis=2,
-    )
-    same = held_pattern[:, :, None] == held_pattern[:, None, :]
-    slot_ids = jnp.arange(slots, dtype=jnp.int32)
-    before = slot_ids[None, :] < slot_ids[:, None]
-    live = jnp.logical_not(jnp.any(same & before[None], axis=2)).astype(jnp.int32)
-    diag = (held_pattern == held_seq[:, None]).astype(jnp.int32)
-    sub = store % 2
-    dev = store // 2
-    core = dev % 2
-    yh = (dev // 2) % 2
-    xi = dev // 4
-    half = jnp.bitwise_xor(core, my_core)
-    row = xi * 1024 + yh * 512 + sub * BLK
-    part_row = xi * 1024 + jnp.bitwise_xor(yh, my_y) * 512 + sub * BLK
-    kind = live * (1 + diag)
-    tables = [half, row, kind, part_row]
-    return jnp.concatenate([t.reshape(-1) for t in tables]).astype(jnp.int32)
+def fill_tables(place, bt, pat, inv, tab):
+    per, devs = bt.shape
+    nslot = pat.shape[0]
+    ns = per * nslot
+    ctx, my_y, my_core = (place[i] for i in range(3))
+    for dev in range(devs):
+        for sub in range(per):
+            inv[bt[sub, dev]] = dev * per + sub
+    for b in range(per):
+        seq = bt[b, ctx]
+        keys = [pat[j, seq] for j in range(nslot)]
+        for j in range(nslot):
+            dead = jnp.int32(0)
+            for i in range(j):
+                dead = dead | (keys[i] == keys[j]).astype(jnp.int32)
+            store = inv[keys[j]]
+            sub = store & 1
+            core = (store >> 1) & 1
+            yh = (store >> 2) & 1
+            xi = store >> 3
+            away = yh ^ my_y
+            t = b * nslot + j
+            tab[t] = core ^ my_core
+            tab[ns + t] = xi * 1024 + yh * 512 + sub * BLK
+            tab[2 * ns + t] = (1 - dead) * (1 + (keys[j] == seq).astype(jnp.int32))
+            tab[3 * ns + t] = xi * 1024 + away * 512 + sub * BLK
 
 
 def load_keys(b, nslot, ns, tab, kva_ref, kvb_ref, kg, vg):
@@ -68,8 +64,8 @@
 
 
 def part_kernel(
-    tab, q_ref, g_ref, kva_ref, kvb_ref, pa_ref, pb_ref, p_ref, ds_ref,
-    kg, vg, bias, qs, gs, s_sc, gp_sc, p_sc, ds_sc, acc_a, acc_b,
+    place, bt, pat, q_ref, g_ref, kva_ref, kvb_ref, pa_ref, pb_ref, p_ref, ds_ref,
+    kg, vg, bias, qs, gs, s_sc, gp_sc, p_sc, ds_sc, acc_a, acc_b, inv, tab,
 ):
     nslot = kg.shape[0] // BLK
     per = q_ref.shape[0] // BLK
@@ -80,6 +76,7 @@
     c2 = scale * math.log2(math.e)
     nt = (((1,), (1,)), ((), ()))
     tn = (((0,), (0,)), ((), ()))
+    fill_tables(place, bt, pat, inv, tab)
     acc_a[...] = jnp.zeros_like(acc_a)
     acc_b[...] = jnp.zeros_like(acc_b)
 
@@ -140,12 +137,14 @@
     pb_ref[...] = acc_b[...].astype(jnp.bfloat16)
 
 
-def row_kernel(tab, p_ref, ds_ref, kva_ref, kvb_ref, att_ref, qg_ref, kg, vg):
+def row_kernel(place, bt, pat, p_ref, ds_ref, kva_ref, kvb_ref, att_ref, qg_ref, kg, vg, inv, tab):
     nslot = kg.shape[0] // BLK
     per = att_ref.shape[0] // BLK
     heads = att_ref.shape[1] // D
     stacked = heads * BLK
     scale = D ** -0.5
+
+    fill_tables(place, bt, pat, inv, tab)
 
     def one_block(b, _):
         load_keys(b, nslot, per * nslot, tab, kva_ref, kvb_ref, kg, vg)
@@ -167,7 +166,8 @@
 SM = pl.BlockSpec(memory_space=pltpu.SMEM)
 
 
-def parts(tab, q, g, kva, kvb, nslot):
+def parts(place, bt, pat, q, g, kva, kvb):
+    nslot = pat.shape[0]
     per = q.shape[0] // BLK
     stacked = q.shape[1] // D * BLK
     bf, f32 = jnp.bfloat16, jnp.float32
@@ -177,7 +177,7 @@
     return pl.pallas_call(
         part_kernel,
         out_shape=tuple(jax.ShapeDtypeStruct(s, bf) for s in shapes),
-        in_specs=[SM, VM, VM, VM, VM],
+        in_specs=[SM] * 3 + [VM] * 4,
         out_specs=(VM, VM, VM, VM),
         scratch_shapes=[
             pltpu.VMEM((keys, D), bf),
@@ -191,30 +191,38 @@
             pltpu.VMEM((stacked, keys), bf),
             pltpu.VMEM(kva.shape, f32),
             pltpu.VMEM(kvb.shape, f32),
+            pltpu.SMEM((bt.shape[0] * bt.shape[1],), jnp.int32),
+            pltpu.SMEM((4 * per * nslot,), jnp.int32),
         ],
         compiler_params=pltpu.CompilerParams(vmem_limit_bytes=VMEM_PARTS << 20),
         cost_estimate=pl.CostEstimate(
             flops=8 * D * work, transcendentals=work, bytes_accessed=6 << 20
         ),
         name="parts",
-    )(tab, q, g, kva, kvb)
-
-
-def rows(tab, p, ds, kva, kvb, shape, nslot):
+    )(place, bt, pat, q, g, kva, kvb)
+
+
+def rows(place, bt, pat, p, ds, kva, kvb, shape):
+    nslot = pat.shape[0]
     bf = jnp.bfloat16
     keys = nslot * BLK
     return pl.pallas_call(
         row_kernel,
         out_shape=tuple(jax.ShapeDtypeStruct(shape, bf) for _ in range(2)),
-        in_specs=[SM, VM, VM, VM, VM],
+        in_specs=[SM] * 3 + [VM] * 4,
         out_specs=(VM, VM),
-        scratch_shapes=[pltpu.VMEM((keys, D), bf), pltpu.VMEM((keys, D), bf)],
+        scratch_shapes=[
+            pltpu.VMEM((keys, D), bf),
+            pltpu.VMEM((keys, D), bf),
+            pltpu.SMEM((bt.shape[0] * bt.shape[1],), jnp.int32),
+            pltpu.SMEM((4 * bt.shape[0] * nslot,), jnp.int32),
+        ],
         compiler_params=pltpu.CompilerParams(vmem_limit_bytes=VMEM_ROWS << 20),
         cost_estimate=pl.CostEstimate(
             flops=4 * D * p.shape[0] * keys, transcendentals=0, bytes_accessed=6 << 20
         ),
         name="rows",
-    )(tab, p, ds, kva, kvb)
+    )(place, bt, pat, p, ds, kva, kvb)
 
 
 def per_device(query_rows, key_rows, value_rows, out_grad, block_table, pattern):
@@ -222,7 +230,6 @@
     my_y = lax.axis_index("yh")
     my_core = lax.axis_index("core")
     ctx = my_x * (NY * NC) + my_y * NC + my_core
-    held_seq = lax.dynamic_index_in_dim(block_table, ctx, 0, keepdims=False)
     f32 = jnp.float32
     bf = jnp.bfloat16
     own = jnp.concatenate([key_rows, value_rows], axis=0)
@@ -232,13 +239,13 @@
         jnp.broadcast_to(pair[None], (NX, n, D)), "x", 0, 0, tiled=True
     ).reshape(NX * n, D)
     kvb = lax.ppermute(kva, "core", SWAP)
-    tab = slot_tables(block_table, pattern, held_seq, my_y, my_core)
-    nslot = pattern.shape[1]
-    part_a, part_b, prob, grad_score = parts(tab, query_rows, out_grad, kva, kvb, nslot)
+    place = jnp.stack([ctx, my_y, my_core]).astype(jnp.int32)
+    bt, pat = block_table.T, pattern.T
+    part_a, part_b, prob, grad_score = parts(place, bt, pat, query_rows, out_grad, kva, kvb)
     other = lax.ppermute(part_b, "core", SWAP)
     both = (part_a.astype(f32) + other.astype(f32)).astype(bf).reshape(NX, n, D)
     both, prob, grad_score = lax.optimization_barrier((both, prob, grad_score))
-    attended, query_grad = rows(tab, prob, grad_score, kva, kvb, query_rows.shape, nslot)
+    attended, query_grad = rows(place, bt, pat, prob, grad_score, kva, kvb, query_rows.shape)
     from_x = lax.all_to_all(both, "x", 0, 0, tiled=True)
     over_x = jnp.sum(from_x.astype(f32), axis=0)
     from_y = lax.ppermute(over_x[n // 2:].astype(bf), "yh", SWAP)

time: 86.6 us -> 84.9 us (0.980)
  blocking collectives: 29.4 us -> 50 us
  waiting for transfers between devices: 23.4 us -> 8.94 us
  starting transfers between devices: 11.8 us -> 6.1 us
  local copies, waits for them, and re-layouts: 2.72 us -> 0.83 us
  other arithmetic: 2.48 us -> 1.5 us
    all_to_all x0 -> x1, blocking collectives: none -> 20.7 us  [per_device(): lax.all_to_all(jnp.broadcast_to(pair[None], (NX, n, D)), 'x', 0, 0, tiled...]
    all_to_all x1 -> x0, waiting for transfers between devices: 14.3 us -> none  [per_device(): lax.all_to_all(jnp.broadcast_to(pair[None], (NX, n, D)), 'x', 0, 0, tiled...]
    all_to_all x1 -> x0, starting transfers between devices: 5.7 us -> none  [per_device(): lax.all_to_all(jnp.broadcast_to(pair[None], (NX, n, D)), 'x', 0, 0, tiled...]
    ppermute x1, waiting for transfers between devices: 5.12 us -> 3.89 us  [per_device(): from_y = lax.ppermute(over_x[n // 2:].astype(bf), 'yh', SWAP)]
    ppermute x1, waiting for transfers between devices: 1.53 us -> 2.54 us  [per_device(): kvb = lax.ppermute(kva, 'core', SWAP)]
    broadcast_in_dim x1, local copies, waits for them, and re-layouts: 1.13 us -> 0.14 us  [per_device(): jnp.broadcast_to(pair[None], (NX, n, D))]
  transfers between devices with their start and end apart: 4 -> 3, of which waited for: 4 -> 3; matrix products, arithmetic and copies ran while one was open for 2% -> 0% of each run, Pallas kernels for 6% -> 6%
where the time goes in v3:
time: 84.9 us; the launch traced here: 84.6 us
  blocking collectives  50 us (59%)
  Pallas kernels  16.4 us (19%)
  waiting for transfers between devices  8.94 us (11%)
  starting transfers between devices  6.1 us (7%)
  other arithmetic  1.5 us (2%)
    all_to_all x1, blocking collectives, per_device(): lax.all_to_all(jnp.broadcast_to(pair[None], (NX, n, D)), 'x', 0, 0, tiled...  20.7 us
    all_to_all x1, blocking collectives, per_device(): from_x = lax.all_to_all(both, 'x', 0, 0, tiled=True)  18.1 us
    all_gather x1, blocking collectives, per_device(): pair = lax.all_gather(own, 'yh', axis=0, tiled=True)  11.3 us
    pallas_call x1, Pallas kernels, parts(): pl.pallas_call(part_kernel, out_shape=tuple((jax.ShapeDtypeStruct(s, bf)...  11.1 us
    pallas_call x1, Pallas kernels, rows(): pl.pallas_call(row_kernel, out_shape=tuple((jax.ShapeDtypeStruct(shape, b...  5.32 us
    ppermute x1, waiting for transfers between devices, per_device(): from_y = lax.ppermute(over_x[n // 2:].astype(bf), 'yh', SWAP)  3.89 us
    ppermute x1, waiting for transfers between devices, per_device(): kvb = lax.ppermute(kva, 'core', SWAP)  2.54 us
    ppermute x1, waiting for transfers between devices, per_device(): other = lax.ppermute(part_b, 'core', SWAP)  2.51 us
  transfers between devices with their start and end apart: 3, of which 3 were waited for; matrix products, arithmetic and copies ran while one was open for 0% of the time, Pallas kernels for 6%

profile of v3, /device:TPU:16, one launch (start us, length us, event | category | flops | bytes accessed | tf_op | source)
XLA Modules:
  0.0 84.6 jit_solution(14156890373449994520)
XLA Ops:
  0.6 0.0 copy-start
  0.6 0.0 copy-start.1
  0.7 0.0 copy-start.3
  0.7 0.0 copy-start.2
  0.7 1.0 %pad_maximum_fusion = bf16[512,128]{1,0:T(8,128)(2,1)S(1)} fusion(bf16[256,128]{1,0:T(8,128)(2,1)} %param.8, bf16[256,128]{1,0:T(8,128)(2,1)} %param.7), kind=kLoop, calls=%fused_computation.5 | loop fusion | flops 262144 | bytes 262144 | tf_op jit(solution)/shard_map/concatenate | solution.py:235
  1.6 11.3 %all_gather.3 = bf16[1024,128]{1,0:T(8,128)(2,1)S(1)} all-gather(bf16[512,128]{1,0:T(8,128)(2,1)S(1)} %pad_maximum_fusion), channel_id=1, replica_groups=mesh['dp'=4,'head'=8,'x'=4,'yh'=2,'core'=2] {'yh'}, dimensions={0}, use_global_device_ids=true | all-gather | bytes 393216 | tf_op jit(solution)/shard_map/all_gather | solution.py:236
  12.9 0.1 broadcast_in_dim.2
  13.0 20.7 %all_to_all.10 = bf16[4,1024,128]{2,1,0:T(8,128)(2,1)S(1)} all-to-all(bf16[4,1024,128]{2,1,0:T(8,128)(2,1)S(1)} %broadcast_in_dim.2), channel_id=1, replica_groups=mesh['dp'=4,'head'=8,'x'=4,'yh'=2,'core'=2] {'x'}, dimensions={0} | all-to-all | bytes 2097152 | tf_op jit(solution)/shard_map/all_to_all | solution.py:238
  33.7 1.9 %collective-permute-start = (bf16[4096,128]{1,0:T(8,128)(2,1)S(1)}, bf16[4096,128]{1,0:T(8,128)(2,1)S(1)}, u32[]{:S(2)}, u32[]{:S(2)}) collective-permute-start(bf16[4096,128]{1,0:T(8,128)(2,1)S(1)} %bitcast.7), channel_id=1, source_target_pairs={{0,1},{1,0},{2,3},{3,2},{4,5},{5,4},{6,7},{7,6},{8,9},{9,8},{10,11... | collective-permute-start | bytes 3145736 | tf_op jit(solution)/shard_map/ppermute | solution.py:241
  35.6 0.1 pad_add_fusion.place
  35.7 2.5 %collective-permute-done.kvb_ref = bf16[4096,128]{1,0:T(8,128)(2,1)S(1)} collective-permute-done((bf16[4096,128]{1,0:T(8,128)(2,1)S(1)}, bf16[4096,128]{1,0:T(8,128)(2,1)S(1)}, u32[]{:S(2)}, u32[]{:S(2)}) %collective-permute-start) | collective-permute-done | bytes 1048608 | tf_op jit(solution)/shard_map/ppermute | solution.py:241
  38.3 0.0 copy-done
  38.3 0.0 copy-done.1
  38.3 0.0 copy-done.2
  38.3 11.1 %parts.1 = (bf16[4096,128]{1,0:T(8,128)(2,1)S(1)}, bf16[4096,128]{1,0:T(8,128)(2,1)S(1)}, bf16[2048,1280]{1,0:T(8,128)(2,1)S(1)}, bf16[2048,1280]{1,0:T(8,128)(2,1)S(1)}) custom-call(s32[3]{0:T(128)S(1)} %pad_add_fusion.place, s32[2,16]{1,0:T(2,128)S(1)} %bitcast.12, s32[10,32]{1,0:T(8,128)S(1)} %bitcast.10, bf16[256,1024]{1,0:T(8,128)(2,1)S(1)} %copy-done.2, ...), custom_call_target="tpu_custom_call" | custom-call | flops 2684354560 | bytes 6291456 | tf_op jit(solution)/shard_map/parts/pallas_call | solution.py:177
  49.4 2.0 %collective-permute-start.1 = (bf16[4096,128]{1,0:T(8,128)(2,1)S(1)}, bf16[4096,128]{1,0:T(8,128)(2,1)S(1)}, u32[]{:S(2)}, u32[]{:S(2)}) collective-permute-start(bf16[4096,128]{1,0:T(8,128)(2,1)S(1)} %get-tuple-element.14), channel_id=1, source_target_pairs={{0,1},{1,0},{2,3},{3,2},{4,5},{5,4},{6,7},{7,6},{8,9},{9,8},{10,11... | collective-permute-start | bytes 3145736 | tf_op jit(solution)/shard_map/ppermute | solution.py:245
  51.5 2.5 %collective-permute-done.1 = bf16[4096,128]{1,0:T(8,128)(2,1)S(1)} collective-permute-done((bf16[4096,128]{1,0:T(8,128)(2,1)S(1)}, bf16[4096,128]{1,0:T(8,128)(2,1)S(1)}, u32[]{:S(2)}, u32[]{:S(2)}) %collective-permute-start.1) | collective-permute-done | bytes 1048608 | tf_op jit(solution)/shard_map/ppermute | solution.py:245
  54.0 0.3 add_convert_fusion
  54.2 18.1 %all_to_all.11 = bf16[4,1024,128]{2,1,0:T(8,128)(2,1)S(1)} all-to-all(bf16[4,1024,128]{2,1,0:T(8,128)(2,1)S(1)} %bitcast.14), channel_id=1, replica_groups=mesh['dp'=4,'head'=8,'x'=4,'yh'=2,'core'=2] {'x'}, dimensions={0} | all-to-all | bytes 2097152 | tf_op jit(solution)/shard_map/all_to_all | solution.py:249
  72.3 0.1 convert_reduce_fusion
  72.5 2.2 %collective-permute-start.2 = (bf16[512,128]{1,0:T(8,128)(2,1)S(1)}, bf16[512,128]{1,0:T(8,128)(2,1)S(1)}, u32[]{:S(2)}, u32[]{:S(2)}) collective-permute-start(bf16[512,128]{1,0:T(8,128)(2,1)S(1)} %slice.25), channel_id=1, source_target_pairs={{0,2},{2,0},{1,3},{3,1},{4,6},{6,4},{5,7},{7,5},{8,10},{10,8},{9,1... | collective-permute-start | bytes 393224 | tf_op jit(solution)/shard_map/ppermute | solution.py:251
  74.7 5.3 %rows.1 = (bf16[256,1024]{1,0:T(8,128)(2,1)}, bf16[256,1024]{1,0:T(8,128)(2,1)}) custom-call(s32[3]{0:T(128)S(1)} %pad_add_fusion.place, s32[2,16]{1,0:T(2,128)S(1)} %bitcast.13, s32[10,32]{1,0:T(8,128)S(1)} %bitcast.11, bf16[2048,1280]{1,0:T(8,128)(2,1)S(1)} %get-tuple-element.17.p_ref, bf16[2048,1280]{1,0:T(8,128)(2,1)S(1)} %get-tuple-element.18.ds_ref, ...), custom_call_target="tpu_custom_call" | custom-call | flops 1342177280 | bytes 6291456 | tf_op jit(solution)/shard_map/rows/pallas_call | solution.py:209
  80.0 3.9 %collective-permute-done.2 = bf16[512,128]{1,0:T(8,128)(2,1)S(1)} collective-permute-done((bf16[512,128]{1,0:T(8,128)(2,1)S(1)}, bf16[512,128]{1,0:T(8,128)(2,1)S(1)}, u32[]{:S(2)}, u32[]{:S(2)}) %collective-permute-start.2) | collective-permute-done | bytes 131104 | tf_op jit(solution)/shard_map/ppermute | solution.py:251
  83.9 0.7 fusion.1
  (3 shorter events, 0.0 us)
Async XLA Ops:
  0.6 37.6 %copy-start = (s32[32,10]{0,1:T(8,128)S(1)}, s32[32,10]{0,1:T(8,128)}, u32[]{:S(2)}) copy-start(s32[32,10]{0,1:T(8,128)} %param.11) | copy-start | bytes 3844
  0.6 37.6 %copy-start.1 = (s32[16,2]{0,1:T(2,128)S(1)}, s32[16,2]{0,1:T(2,128)}, u32[]{:S(2)}) copy-start(s32[16,2]{0,1:T(2,128)} %param.10) | copy-start | bytes 388
  0.7 37.6 %copy-start.3 = (bf16[256,1024]{1,0:T(8,128)(2,1)S(1)}, bf16[256,1024]{1,0:T(8,128)(2,1)}, u32[]{:S(2)}) copy-start(bf16[256,1024]{1,0:T(8,128)(2,1)} %g_ref.1) | copy-start | bytes 1572868
  0.7 37.6 %copy-start.2 = (bf16[256,1024]{1,0:T(8,128)(2,1)S(1)}, bf16[256,1024]{1,0:T(8,128)(2,1)}, u32[]{:S(2)}) copy-start(bf16[256,1024]{1,0:T(8,128)(2,1)} %q_ref.1) | copy-start | bytes 1572868
  33.7 4.5 %collective-permute-start = (bf16[4096,128]{1,0:T(8,128)(2,1)S(1)}, bf16[4096,128]{1,0:T(8,128)(2,1)S(1)}, u32[]{:S(2)}, u32[]{:S(2)}) collective-permute-start(bf16[4096,128]{1,0:T(8,128)(2,1)S(1)} %bitcast.7), channel_id=1, source_target_pairs={{0,1},{1,0},{2,3},{3,2},{4,5},{5,4},{6,7},{7,6},{8,9},{9,8},{10,11... | collective-permute-start | bytes 3145736 | tf_op jit(solution)/shard_map/ppermute | solution.py:241
  49.4 4.6 %collective-permute-start.1 = (bf16[4096,128]{1,0:T(8,128)(2,1)S(1)}, bf16[4096,128]{1,0:T(8,128)(2,1)S(1)}, u32[]{:S(2)}, u32[]{:S(2)}) collective-permute-start(bf16[4096,128]{1,0:T(8,128)(2,1)S(1)} %get-tuple-element.14), channel_id=1, source_target_pairs={{0,1},{1,0},{2,3},{3,2},{4,5},{5,4},{6,7},{7,6},{8,9},{9,8},{10,11... | collective-permute-start | bytes 3145736 | tf_op jit(solution)/shard_map/ppermute | solution.py:245
  72.5 11.4 %collective-permute-start.2 = (bf16[512,128]{1,0:T(8,128)(2,1)S(1)}, bf16[512,128]{1,0:T(8,128)(2,1)S(1)}, u32[]{:S(2)}, u32[]{:S(2)}) collective-permute-start(bf16[512,128]{1,0:T(8,128)(2,1)S(1)} %slice.25), channel_id=1, source_target_pairs={{0,2},{2,0},{1,3},{3,1},{4,6},{6,4},{5,7},{7,5},{8,10},{10,8},{9,1... | collective-permute-start | bytes 393224 | tf_op jit(solution)/shard_map/ppermute | solution.py:251

commit v4 on v3

--- a/solution.py
+++ b/solution.py
@@ -110,8 +110,8 @@
         mine = pl.ds(s0, stacked)
         p_ref[mine, :] = p_sc[...]
         ds_ref[mine, :] = ds_sc[...]
-        dk_all = lax.dot_general(ds_sc[...], qs[...], tn, preferred_element_type=jnp.float32) * scale
-        dv_all = lax.dot_general(p_sc[...], gs[...], tn, preferred_element_type=jnp.float32)
+        dk_all = lax.dot_general(qs[...], ds_sc[...], tn, preferred_element_type=jnp.float32).T * scale
+        dv_all = lax.dot_general(gs[...], p_sc[...], tn, preferred_element_type=jnp.float32).T
         for j in range(nslot):
             t = b * nslot + j
             half = tab[t]

time: 84.9 us -> 84.1 us (level)
  no operation moved by 1% of the time
where the time goes in v4:
time: 84.1 us; the launch traced here: 83.8 us
  blocking collectives  50 us (59%)
  Pallas kernels  15.7 us (19%)
  waiting for transfers between devices  8.94 us (11%)
  starting transfers between devices  6.1 us (7%)
  other arithmetic  1.5 us (2%)
    all_to_all x1, blocking collectives, per_device(): lax.all_to_all(jnp.broadcast_to(pair[None], (NX, n, D)), 'x', 0, 0, tiled...  20.7 us
    all_to_all x1, blocking collectives, per_device(): from_x = lax.all_to_all(both, 'x', 0, 0, tiled=True)  18.1 us
    all_gather x1, blocking collectives, per_device(): pair = lax.all_gather(own, 'yh', axis=0, tiled=True)  11.3 us
    pallas_call x1, Pallas kernels, parts(): pl.pallas_call(part_kernel, out_shape=tuple((jax.ShapeDtypeStruct(s, bf)...  10.4 us
    pallas_call x1, Pallas kernels, rows(): pl.pallas_call(row_kernel, out_shape=tuple((jax.ShapeDtypeStruct(shape, b...  5.32 us
    ppermute x1, waiting for transfers between devices, per_device(): from_y = lax.ppermute(over_x[n // 2:].astype(bf), 'yh', SWAP)  3.88 us
    ppermute x1, waiting for transfers between devices, per_device(): kvb = lax.ppermute(kva, 'core', SWAP)  2.54 us
    ppermute x1, waiting for transfers between devices, per_device(): other = lax.ppermute(part_b, 'core', SWAP)  2.52 us
  transfers between devices with their start and end apart: 3, of which 3 were waited for; matrix products, arithmetic and copies ran while one was open for 0% of the time, Pallas kernels for 6%

profile of v4, /device:TPU:16, one launch (start us, length us, event | category | flops | bytes accessed | tf_op | source)
XLA Modules:
  0.0 83.8 jit_solution(11932111260277908640)
XLA Ops:
  0.6 0.0 copy-start
  0.6 0.0 copy-start.1
  0.7 0.0 copy-start.3
  0.7 0.0 copy-start.2
  0.7 1.0 %pad_maximum_fusion = bf16[512,128]{1,0:T(8,128)(2,1)S(1)} fusion(bf16[256,128]{1,0:T(8,128)(2,1)} %param.8, bf16[256,128]{1,0:T(8,128)(2,1)} %param.7), kind=kLoop, calls=%fused_computation.5 | loop fusion | flops 262144 | bytes 262144 | tf_op jit(solution)/shard_map/concatenate | solution.py:235
  1.6 11.3 %all_gather.3 = bf16[1024,128]{1,0:T(8,128)(2,1)S(1)} all-gather(bf16[512,128]{1,0:T(8,128)(2,1)S(1)} %pad_maximum_fusion), channel_id=1, replica_groups=mesh['dp'=4,'head'=8,'x'=4,'yh'=2,'core'=2] {'yh'}, dimensions={0}, use_global_device_ids=true | all-gather | bytes 393216 | tf_op jit(solution)/shard_map/all_gather | solution.py:236
  12.9 0.1 broadcast_in_dim.2
  13.0 20.7 %all_to_all.10 = bf16[4,1024,128]{2,1,0:T(8,128)(2,1)S(1)} all-to-all(bf16[4,1024,128]{2,1,0:T(8,128)(2,1)S(1)} %broadcast_in_dim.2), channel_id=1, replica_groups=mesh['dp'=4,'head'=8,'x'=4,'yh'=2,'core'=2] {'x'}, dimensions={0} | all-to-all | bytes 2097152 | tf_op jit(solution)/shard_map/all_to_all | solution.py:238
  33.7 1.9 %collective-permute-start = (bf16[4096,128]{1,0:T(8,128)(2,1)S(1)}, bf16[4096,128]{1,0:T(8,128)(2,1)S(1)}, u32[]{:S(2)}, u32[]{:S(2)}) collective-permute-start(bf16[4096,128]{1,0:T(8,128)(2,1)S(1)} %bitcast.7), channel_id=1, source_target_pairs={{0,1},{1,0},{2,3},{3,2},{4,5},{5,4},{6,7},{7,6},{8,9},{9,8},{10,11... | collective-permute-start | bytes 3145736 | tf_op jit(solution)/shard_map/ppermute | solution.py:241
  35.6 0.1 pad_add_fusion.place
  35.7 2.5 %collective-permute-done.kvb_ref = bf16[4096,128]{1,0:T(8,128)(2,1)S(1)} collective-permute-done((bf16[4096,128]{1,0:T(8,128)(2,1)S(1)}, bf16[4096,128]{1,0:T(8,128)(2,1)S(1)}, u32[]{:S(2)}, u32[]{:S(2)}) %collective-permute-start) | collective-permute-done | bytes 1048608 | tf_op jit(solution)/shard_map/ppermute | solution.py:241
  38.3 0.0 copy-done
  38.3 0.0 copy-done.1
  38.3 0.0 copy-done.2
  38.3 10.4 %parts.1 = (bf16[4096,128]{1,0:T(8,128)(2,1)S(1)}, bf16[4096,128]{1,0:T(8,128)(2,1)S(1)}, bf16[2048,1280]{1,0:T(8,128)(2,1)S(1)}, bf16[2048,1280]{1,0:T(8,128)(2,1)S(1)}) custom-call(s32[3]{0:T(128)S(1)} %pad_add_fusion.place, s32[2,16]{1,0:T(2,128)S(1)} %bitcast.12, s32[10,32]{1,0:T(8,128)S(1)} %bitcast.10, bf16[256,1024]{1,0:T(8,128)(2,1)S(1)} %copy-done.2, ...), custom_call_target="tpu_custom_call" | custom-call | flops 2684354560 | bytes 6291456 | tf_op jit(solution)/shard_map/parts/pallas_call | solution.py:177
  48.7 2.0 %collective-permute-start.1 = (bf16[4096,128]{1,0:T(8,128)(2,1)S(1)}, bf16[4096,128]{1,0:T(8,128)(2,1)S(1)}, u32[]{:S(2)}, u32[]{:S(2)}) collective-permute-start(bf16[4096,128]{1,0:T(8,128)(2,1)S(1)} %get-tuple-element.14), channel_id=1, source_target_pairs={{0,1},{1,0},{2,3},{3,2},{4,5},{5,4},{6,7},{7,6},{8,9},{9,8},{10,11... | collective-permute-start | bytes 3145736 | tf_op jit(solution)/shard_map/ppermute | solution.py:245
  50.7 2.5 %collective-permute-done.1 = bf16[4096,128]{1,0:T(8,128)(2,1)S(1)} collective-permute-done((bf16[4096,128]{1,0:T(8,128)(2,1)S(1)}, bf16[4096,128]{1,0:T(8,128)(2,1)S(1)}, u32[]{:S(2)}, u32[]{:S(2)}) %collective-permute-start.1) | collective-permute-done | bytes 1048608 | tf_op jit(solution)/shard_map/ppermute | solution.py:245
  53.2 0.3 add_convert_fusion
  53.5 18.1 %all_to_all.11 = bf16[4,1024,128]{2,1,0:T(8,128)(2,1)S(1)} all-to-all(bf16[4,1024,128]{2,1,0:T(8,128)(2,1)S(1)} %bitcast.14), channel_id=1, replica_groups=mesh['dp'=4,'head'=8,'x'=4,'yh'=2,'core'=2] {'x'}, dimensions={0} | all-to-all | bytes 2097152 | tf_op jit(solution)/shard_map/all_to_all | solution.py:249
  71.6 0.1 convert_reduce_fusion
  71.8 2.2 %collective-permute-start.2 = (bf16[512,128]{1,0:T(8,128)(2,1)S(1)}, bf16[512,128]{1,0:T(8,128)(2,1)S(1)}, u32[]{:S(2)}, u32[]{:S(2)}) collective-permute-start(bf16[512,128]{1,0:T(8,128)(2,1)S(1)} %slice.25), channel_id=1, source_target_pairs={{0,2},{2,0},{1,3},{3,1},{4,6},{6,4},{5,7},{7,5},{8,10},{10,8},{9,1... | collective-permute-start | bytes 393224 | tf_op jit(solution)/shard_map/ppermute | solution.py:251
  73.9 5.3 %rows.1 = (bf16[256,1024]{1,0:T(8,128)(2,1)}, bf16[256,1024]{1,0:T(8,128)(2,1)}) custom-call(s32[3]{0:T(128)S(1)} %pad_add_fusion.place, s32[2,16]{1,0:T(2,128)S(1)} %bitcast.13, s32[10,32]{1,0:T(8,128)S(1)} %bitcast.11, bf16[2048,1280]{1,0:T(8,128)(2,1)S(1)} %get-tuple-element.17.p_ref, bf16[2048,1280]{1,0:T(8,128)(2,1)S(1)} %get-tuple-element.18.ds_ref, ...), custom_call_target="tpu_custom_call" | custom-call | flops 1342177280 | bytes 6291456 | tf_op jit(solution)/shard_map/rows/pallas_call | solution.py:209
  79.3 3.9 %collective-permute-done.2 = bf16[512,128]{1,0:T(8,128)(2,1)S(1)} collective-permute-done((bf16[512,128]{1,0:T(8,128)(2,1)S(1)}, bf16[512,128]{1,0:T(8,128)(2,1)S(1)}, u32[]{:S(2)}, u32[]{:S(2)}) %collective-permute-start.2) | collective-permute-done | bytes 131104 | tf_op jit(solution)/shard_map/ppermute | solution.py:251
  83.2 0.7 fusion.1
  (3 shorter events, 0.0 us)
Async XLA Ops:
  0.6 37.6 %copy-start = (s32[32,10]{0,1:T(8,128)S(1)}, s32[32,10]{0,1:T(8,128)}, u32[]{:S(2)}) copy-start(s32[32,10]{0,1:T(8,128)} %param.11) | copy-start | bytes 3844
  0.6 37.6 %copy-start.1 = (s32[16,2]{0,1:T(2,128)S(1)}, s32[16,2]{0,1:T(2,128)}, u32[]{:S(2)}) copy-start(s32[16,2]{0,1:T(2,128)} %param.10) | copy-start | bytes 388
  0.7 37.6 %copy-start.3 = (bf16[256,1024]{1,0:T(8,128)(2,1)S(1)}, bf16[256,1024]{1,0:T(8,128)(2,1)}, u32[]{:S(2)}) copy-start(bf16[256,1024]{1,0:T(8,128)(2,1)} %g_ref.1) | copy-start | bytes 1572868
  0.7 37.6 %copy-start.2 = (bf16[256,1024]{1,0:T(8,128)(2,1)S(1)}, bf16[256,1024]{1,0:T(8,128)(2,1)}, u32[]{:S(2)}) copy-start(bf16[256,1024]{1,0:T(8,128)(2,1)} %q_ref.1) | copy-start | bytes 1572868
  33.7 4.5 %collective-permute-start = (bf16[4096,128]{1,0:T(8,128)(2,1)S(1)}, bf16[4096,128]{1,0:T(8,128)(2,1)S(1)}, u32[]{:S(2)}, u32[]{:S(2)}) collective-permute-start(bf16[4096,128]{1,0:T(8,128)(2,1)S(1)} %bitcast.7), channel_id=1, source_target_pairs={{0,1},{1,0},{2,3},{3,2},{4,5},{5,4},{6,7},{7,6},{8,9},{9,8},{10,11... | collective-permute-start | bytes 3145736 | tf_op jit(solution)/shard_map/ppermute | solution.py:241
  48.7 4.6 %collective-permute-start.1 = (bf16[4096,128]{1,0:T(8,128)(2,1)S(1)}, bf16[4096,128]{1,0:T(8,128)(2,1)S(1)}, u32[]{:S(2)}, u32[]{:S(2)}) collective-permute-start(bf16[4096,128]{1,0:T(8,128)(2,1)S(1)} %get-tuple-element.14), channel_id=1, source_target_pairs={{0,1},{1,0},{2,3},{3,2},{4,5},{5,4},{6,7},{7,6},{8,9},{9,8},{10,11... | collective-permute-start | bytes 3145736 | tf_op jit(solution)/shard_map/ppermute | solution.py:245
  71.8 11.4 %collective-permute-start.2 = (bf16[512,128]{1,0:T(8,128)(2,1)S(1)}, bf16[512,128]{1,0:T(8,128)(2,1)S(1)}, u32[]{:S(2)}, u32[]{:S(2)}) collective-permute-start(bf16[512,128]{1,0:T(8,128)(2,1)S(1)} %slice.25), channel_id=1, source_target_pairs={{0,2},{2,0},{1,3},{3,1},{4,6},{6,4},{5,7},{7,5},{8,10},{10,8},{9,1... | collective-permute-start | bytes 393224 | tf_op jit(solution)/shard_map/ppermute | solution.py:251

commit v5 on v4

--- a/solution.py
+++ b/solution.py
@@ -17,7 +17,7 @@
 SWAP = [(0, 1), (1, 0)]
 
 
-def fill_tables(place, bt, pat, inv, tab):
+def fill_tables(place, bt, pat, inv, tab, sums):
     per, devs = bt.shape
     nslot = pat.shape[0]
     ns = per * nslot
@@ -28,10 +28,10 @@
     for b in range(per):
         seq = bt[b, ctx]
         keys = [pat[j, seq] for j in range(nslot)]
+        seen = jnp.int32(0)
         for j in range(nslot):
-            dead = jnp.int32(0)
-            for i in range(j):
-                dead = dead | (keys[i] == keys[j]).astype(jnp.int32)
+            dead = lax.shift_right_logical(seen, keys[j]) & 1
+            seen = seen | lax.shift_left(jnp.int32(1), keys[j])
             store = inv[keys[j]]
             sub = store & 1
             core = (store >> 1) & 1
@@ -41,6 +41,8 @@
             t = b * nslot + j
             tab[t] = core ^ my_core
             tab[ns + t] = xi * 1024 + yh * 512 + sub * BLK
+            if not sums:
+                continue
             tab[2 * ns + t] = (1 - dead) * (1 + (keys[j] == seq).astype(jnp.int32))
             tab[3 * ns + t] = xi * 1024 + away * 512 + sub * BLK
 
@@ -76,7 +78,7 @@
     c2 = scale * math.log2(math.e)
     nt = (((1,), (1,)), ((), ()))
     tn = (((0,), (0,)), ((), ()))
-    fill_tables(place, bt, pat, inv, tab)
+    fill_tables(place, bt, pat, inv, tab, True)
     acc_a[...] = jnp.zeros_like(acc_a)
     acc_b[...] = jnp.zeros_like(acc_b)
 
@@ -144,7 +146,7 @@
     stacked = heads * BLK
     scale = D ** -0.5
 
-    fill_tables(place, bt, pat, inv, tab)
+    fill_tables(place, bt, pat, inv, tab, False)
 
     def one_block(b, _):
         load_keys(b, nslot, per * nslot, tab, kva_ref, kvb_ref, kg, vg)

time: 84.1 us -> 84.1 us (level)
  no operation moved by 1% of the time
where the time goes in v5:
time: 84.1 us; the launch traced here: 83.8 us
  blocking collectives  50 us (59%)
  Pallas kernels  15.5 us (18%)
  waiting for transfers between devices  9.12 us (11%)
  starting transfers between devices  6.1 us (7%)
  other arithmetic  1.5 us (2%)
    all_to_all x1, blocking collectives, per_device(): lax.all_to_all(jnp.broadcast_to(pair[None], (NX, n, D)), 'x', 0, 0, tiled...  20.7 us
    all_to_all x1, blocking collectives, per_device(): from_x = lax.all_to_all(both, 'x', 0, 0, tiled=True)  18.1 us
    all_gather x1, blocking collectives, per_device(): pair = lax.all_gather(own, 'yh', axis=0, tiled=True)  11.3 us
    pallas_call x1, Pallas kernels, parts(): pl.pallas_call(part_kernel, out_shape=tuple((jax.ShapeDtypeStruct(s, bf)...  10.4 us
    pallas_call x1, Pallas kernels, rows(): pl.pallas_call(row_kernel, out_shape=tuple((jax.ShapeDtypeStruct(shape, b...  5.15 us
    ppermute x1, waiting for transfers between devices, per_device(): from_y = lax.ppermute(over_x[n // 2:].astype(bf), 'yh', SWAP)  4.06 us
    ppermute x1, waiting for transfers between devices, per_device(): kvb = lax.ppermute(kva, 'core', SWAP)  2.54 us
    ppermute x1, waiting for transfers between devices, per_device(): other = lax.ppermute(part_b, 'core', SWAP)  2.52 us
  transfers between devices with their start and end apart: 3, of which 3 were waited for; matrix products, arithmetic and copies ran while one was open for 0% of the time, Pallas kernels for 6%

profile of v5, /device:TPU:16, one launch (start us, length us, event | category | flops | bytes accessed | tf_op | source)
XLA Modules:
  0.0 83.8 jit_solution(10326608579841142352)
XLA Ops:
  0.6 0.0 copy-start
  0.6 0.0 copy-start.1
  0.7 0.0 copy-start.3
  0.7 0.0 copy-start.2
  0.7 1.0 %pad_maximum_fusion = bf16[512,128]{1,0:T(8,128)(2,1)S(1)} fusion(bf16[256,128]{1,0:T(8,128)(2,1)} %param.8, bf16[256,128]{1,0:T(8,128)(2,1)} %param.7), kind=kLoop, calls=%fused_computation.5 | loop fusion | flops 262144 | bytes 262144 | tf_op jit(solution)/shard_map/concatenate | solution.py:237
  1.6 11.3 %all_gather.3 = bf16[1024,128]{1,0:T(8,128)(2,1)S(1)} all-gather(bf16[512,128]{1,0:T(8,128)(2,1)S(1)} %pad_maximum_fusion), channel_id=1, replica_groups=mesh['dp'=4,'head'=8,'x'=4,'yh'=2,'core'=2] {'yh'}, dimensions={0}, use_global_device_ids=true | all-gather | bytes 393216 | tf_op jit(solution)/shard_map/all_gather | solution.py:238
  12.9 0.1 broadcast_in_dim.2
  13.0 20.7 %all_to_all.10 = bf16[4,1024,128]{2,1,0:T(8,128)(2,1)S(1)} all-to-all(bf16[4,1024,128]{2,1,0:T(8,128)(2,1)S(1)} %broadcast_in_dim.2), channel_id=1, replica_groups=mesh['dp'=4,'head'=8,'x'=4,'yh'=2,'core'=2] {'x'}, dimensions={0} | all-to-all | bytes 2097152 | tf_op jit(solution)/shard_map/all_to_all | solution.py:240
  33.7 1.9 %collective-permute-start = (bf16[4096,128]{1,0:T(8,128)(2,1)S(1)}, bf16[4096,128]{1,0:T(8,128)(2,1)S(1)}, u32[]{:S(2)}, u32[]{:S(2)}) collective-permute-start(bf16[4096,128]{1,0:T(8,128)(2,1)S(1)} %bitcast.7), channel_id=1, source_target_pairs={{0,1},{1,0},{2,3},{3,2},{4,5},{5,4},{6,7},{7,6},{8,9},{9,8},{10,11... | collective-permute-start | bytes 3145736 | tf_op jit(solution)/shard_map/ppermute | solution.py:243
  35.6 0.1 pad_add_fusion.place
  35.7 2.5 %collective-permute-done.kvb_ref = bf16[4096,128]{1,0:T(8,128)(2,1)S(1)} collective-permute-done((bf16[4096,128]{1,0:T(8,128)(2,1)S(1)}, bf16[4096,128]{1,0:T(8,128)(2,1)S(1)}, u32[]{:S(2)}, u32[]{:S(2)}) %collective-permute-start) | collective-permute-done | bytes 1048608 | tf_op jit(solution)/shard_map/ppermute | solution.py:243
  38.3 0.0 copy-done
  38.3 0.0 copy-done.3
  38.3 0.0 copy-done.2
  38.3 10.4 %parts.1 = (bf16[4096,128]{1,0:T(8,128)(2,1)S(1)}, bf16[4096,128]{1,0:T(8,128)(2,1)S(1)}, bf16[2048,1280]{1,0:T(8,128)(2,1)S(1)}, bf16[2048,1280]{1,0:T(8,128)(2,1)S(1)}) custom-call(s32[3]{0:T(128)S(1)} %pad_add_fusion.place, s32[2,16]{1,0:T(2,128)S(1)} %bitcast.12, s32[10,32]{1,0:T(8,128)S(1)} %bitcast.10, bf16[256,1024]{1,0:T(8,128)(2,1)S(1)} %copy-done.2, ...), custom_call_target="tpu_custom_call" | custom-call | flops 2684354560 | bytes 6291456 | tf_op jit(solution)/shard_map/parts/pallas_call | solution.py:179
  48.7 2.0 %collective-permute-start.1 = (bf16[4096,128]{1,0:T(8,128)(2,1)S(1)}, bf16[4096,128]{1,0:T(8,128)(2,1)S(1)}, u32[]{:S(2)}, u32[]{:S(2)}) collective-permute-start(bf16[4096,128]{1,0:T(8,128)(2,1)S(1)} %get-tuple-element.14), channel_id=1, source_target_pairs={{0,1},{1,0},{2,3},{3,2},{4,5},{5,4},{6,7},{7,6},{8,9},{9,8},{10,11... | collective-permute-start | bytes 3145736 | tf_op jit(solution)/shard_map/ppermute | solution.py:247
  50.7 2.5 %collective-permute-done.1 = bf16[4096,128]{1,0:T(8,128)(2,1)S(1)} collective-permute-done((bf16[4096,128]{1,0:T(8,128)(2,1)S(1)}, bf16[4096,128]{1,0:T(8,128)(2,1)S(1)}, u32[]{:S(2)}, u32[]{:S(2)}) %collective-permute-start.1) | collective-permute-done | bytes 1048608 | tf_op jit(solution)/shard_map/ppermute | solution.py:247
  53.2 0.3 add_convert_fusion
  53.5 18.1 %all_to_all.11 = bf16[4,1024,128]{2,1,0:T(8,128)(2,1)S(1)} all-to-all(bf16[4,1024,128]{2,1,0:T(8,128)(2,1)S(1)} %bitcast.14), channel_id=1, replica_groups=mesh['dp'=4,'head'=8,'x'=4,'yh'=2,'core'=2] {'x'}, dimensions={0} | all-to-all | bytes 2097152 | tf_op jit(solution)/shard_map/all_to_all | solution.py:251
  71.6 0.1 convert_reduce_fusion
  71.8 2.2 %collective-permute-start.2 = (bf16[512,128]{1,0:T(8,128)(2,1)S(1)}, bf16[512,128]{1,0:T(8,128)(2,1)S(1)}, u32[]{:S(2)}, u32[]{:S(2)}) collective-permute-start(bf16[512,128]{1,0:T(8,128)(2,1)S(1)} %slice.25), channel_id=1, source_target_pairs={{0,2},{2,0},{1,3},{3,1},{4,6},{6,4},{5,7},{7,5},{8,10},{10,8},{9,1... | collective-permute-start | bytes 393224 | tf_op jit(solution)/shard_map/ppermute | solution.py:253
  73.9 5.1 %rows.1 = (bf16[256,1024]{1,0:T(8,128)(2,1)}, bf16[256,1024]{1,0:T(8,128)(2,1)}) custom-call(s32[3]{0:T(128)S(1)} %pad_add_fusion.place, s32[2,16]{1,0:T(2,128)S(1)} %bitcast.13, s32[10,32]{1,0:T(8,128)S(1)} %bitcast.11, bf16[2048,1280]{1,0:T(8,128)(2,1)S(1)} %get-tuple-element.17.p_ref, bf16[2048,1280]{1,0:T(8,128)(2,1)S(1)} %get-tuple-element.18.ds_ref, ...), custom_call_target="tpu_custom_call" | custom-call | flops 1342177280 | bytes 6291456 | tf_op jit(solution)/shard_map/rows/pallas_call | solution.py:211
  79.1 4.1 %collective-permute-done.2 = bf16[512,128]{1,0:T(8,128)(2,1)S(1)} collective-permute-done((bf16[512,128]{1,0:T(8,128)(2,1)S(1)}, bf16[512,128]{1,0:T(8,128)(2,1)S(1)}, u32[]{:S(2)}, u32[]{:S(2)}) %collective-permute-start.2) | collective-permute-done | bytes 131104 | tf_op jit(solution)/shard_map/ppermute | solution.py:253
  83.2 0.7 fusion.1
  (3 shorter events, 0.0 us)
Async XLA Ops:
  0.6 37.6 %copy-start = (s32[32,10]{0,1:T(8,128)S(1)}, s32[32,10]{0,1:T(8,128)}, u32[]{:S(2)}) copy-start(s32[32,10]{0,1:T(8,128)} %param.11) | copy-start | bytes 3844
  0.6 37.6 %copy-start.1 = (s32[16,2]{0,1:T(2,128)S(1)}, s32[16,2]{0,1:T(2,128)}, u32[]{:S(2)}) copy-start(s32[16,2]{0,1:T(2,128)} %param.10) | copy-start | bytes 388
  0.7 37.6 %copy-start.3 = (bf16[256,1024]{1,0:T(8,128)(2,1)S(1)}, bf16[256,1024]{1,0:T(8,128)(2,1)}, u32[]{:S(2)}) copy-start(bf16[256,1024]{1,0:T(8,128)(2,1)} %g_ref.1) | copy-start | bytes 1572868
  0.7 37.6 %copy-start.2 = (bf16[256,1024]{1,0:T(8,128)(2,1)S(1)}, bf16[256,1024]{1,0:T(8,128)(2,1)}, u32[]{:S(2)}) copy-start(bf16[256,1024]{1,0:T(8,128)(2,1)} %q_ref.1) | copy-start | bytes 1572868
  33.7 4.5 %collective-permute-start = (bf16[4096,128]{1,0:T(8,128)(2,1)S(1)}, bf16[4096,128]{1,0:T(8,128)(2,1)S(1)}, u32[]{:S(2)}, u32[]{:S(2)}) collective-permute-start(bf16[4096,128]{1,0:T(8,128)(2,1)S(1)} %bitcast.7), channel_id=1, source_target_pairs={{0,1},{1,0},{2,3},{3,2},{4,5},{5,4},{6,7},{7,6},{8,9},{9,8},{10,11... | collective-permute-start | bytes 3145736 | tf_op jit(solution)/shard_map/ppermute | solution.py:243
  48.7 4.6 %collective-permute-start.1 = (bf16[4096,128]{1,0:T(8,128)(2,1)S(1)}, bf16[4096,128]{1,0:T(8,128)(2,1)S(1)}, u32[]{:S(2)}, u32[]{:S(2)}) collective-permute-start(bf16[4096,128]{1,0:T(8,128)(2,1)S(1)} %get-tuple-element.14), channel_id=1, source_target_pairs={{0,1},{1,0},{2,3},{3,2},{4,5},{5,4},{6,7},{7,6},{8,9},{9,8},{10,11... | collective-permute-start | bytes 3145736 | tf_op jit(solution)/shard_map/ppermute | solution.py:247
  71.8 11.4 %collective-permute-start.2 = (bf16[512,128]{1,0:T(8,128)(2,1)S(1)}, bf16[512,128]{1,0:T(8,128)(2,1)S(1)}, u32[]{:S(2)}, u32[]{:S(2)}) collective-permute-start(bf16[512,128]{1,0:T(8,128)(2,1)S(1)} %slice.25), channel_id=1, source_target_pairs={{0,2},{2,0},{1,3},{3,1},{4,6},{6,4},{5,7},{7,5},{8,10},{10,8},{9,1... | collective-permute-start | bytes 393224 | tf_op jit(solution)/shard_map/ppermute | solution.py:253

commit v6 on v5

--- a/solution.py
+++ b/solution.py
@@ -251,8 +251,10 @@
     from_x = lax.all_to_all(both, "x", 0, 0, tiled=True)
     over_x = jnp.sum(from_x.astype(f32), axis=0)
     from_y = lax.ppermute(over_x[n // 2:].astype(bf), "yh", SWAP)
-    total = (over_x[: n // 2] + from_y.astype(f32)).astype(bf)
-    return attended, query_grad, total[: n // 4], total[n // 4:]
+    q = n // 4
+    key_grad = (over_x[:q] + from_y[:q].astype(f32)).astype(bf)
+    value_grad = (over_x[q:2 * q] + from_y[q:].astype(f32)).astype(bf)
+    return attended, query_grad, key_grad, value_grad
 
 
 def solution(mesh):

time: 84.1 us -> 84.1 us (level)
  no operation moved by 1% of the time
where the time goes in v6:
time: 84.1 us; the launch traced here: 83.8 us
  blocking collectives  50 us (59%)
  Pallas kernels  15.5 us (18%)
  waiting for transfers between devices  9.12 us (11%)
  starting transfers between devices  6.1 us (7%)
  other arithmetic  2.15 us (3%)
    all_to_all x1, blocking collectives, per_device(): lax.all_to_all(jnp.broadcast_to(pair[None], (NX, n, D)), 'x', 0, 0, tiled...  20.7 us
    all_to_all x1, blocking collectives, per_device(): from_x = lax.all_to_all(both, 'x', 0, 0, tiled=True)  18.1 us
    all_gather x1, blocking collectives, per_device(): pair = lax.all_gather(own, 'yh', axis=0, tiled=True)  11.3 us
    pallas_call x1, Pallas kernels, parts(): pl.pallas_call(part_kernel, out_shape=tuple((jax.ShapeDtypeStruct(s, bf)...  10.4 us
    pallas_call x1, Pallas kernels, rows(): pl.pallas_call(row_kernel, out_shape=tuple((jax.ShapeDtypeStruct(shape, b...  5.15 us
    ppermute x1, waiting for transfers between devices, per_device(): from_y = lax.ppermute(over_x[n // 2:].astype(bf), 'yh', SWAP)  4.06 us
    ppermute x1, waiting for transfers between devices, per_device(): kvb = lax.ppermute(kva, 'core', SWAP)  2.54 us
    ppermute x1, waiting for transfers between devices, per_device(): other = lax.ppermute(part_b, 'core', SWAP)  2.52 us
  transfers between devices with their start and end apart: 3, of which 3 were waited for; matrix products, arithmetic and copies ran while one was open for 0% of the time, Pallas kernels for 6%

profile of v6, /device:TPU:16, one launch (start us, length us, event | category | flops | bytes accessed | tf_op | source)
XLA Modules:
  0.0 83.8 jit_solution(13352578899292572639)
XLA Ops:
  0.6 0.0 copy-start
  0.6 0.0 copy-start.1
  0.7 0.0 copy-start.3
  0.7 0.0 copy-start.2
  0.7 1.0 %pad_maximum_fusion = bf16[512,128]{1,0:T(8,128)(2,1)S(1)} fusion(bf16[256,128]{1,0:T(8,128)(2,1)} %param.8, bf16[256,128]{1,0:T(8,128)(2,1)} %param.7), kind=kLoop, calls=%fused_computation.7 | loop fusion | flops 262144 | bytes 262144 | tf_op jit(solution)/shard_map/concatenate | solution.py:237
  1.6 11.3 %all_gather.3 = bf16[1024,128]{1,0:T(8,128)(2,1)S(1)} all-gather(bf16[512,128]{1,0:T(8,128)(2,1)S(1)} %pad_maximum_fusion), channel_id=1, replica_groups=mesh['dp'=4,'head'=8,'x'=4,'yh'=2,'core'=2] {'yh'}, dimensions={0}, use_global_device_ids=true | all-gather | bytes 393216 | tf_op jit(solution)/shard_map/all_gather | solution.py:238
  12.9 0.1 broadcast_in_dim.2
  13.0 20.7 %all_to_all.10 = bf16[4,1024,128]{2,1,0:T(8,128)(2,1)S(1)} all-to-all(bf16[4,1024,128]{2,1,0:T(8,128)(2,1)S(1)} %broadcast_in_dim.2), channel_id=1, replica_groups=mesh['dp'=4,'head'=8,'x'=4,'yh'=2,'core'=2] {'x'}, dimensions={0} | all-to-all | bytes 2097152 | tf_op jit(solution)/shard_map/all_to_all | solution.py:240
  33.7 1.9 %collective-permute-start = (bf16[4096,128]{1,0:T(8,128)(2,1)S(1)}, bf16[4096,128]{1,0:T(8,128)(2,1)S(1)}, u32[]{:S(2)}, u32[]{:S(2)}) collective-permute-start(bf16[4096,128]{1,0:T(8,128)(2,1)S(1)} %bitcast.7), channel_id=1, source_target_pairs={{0,1},{1,0},{2,3},{3,2},{4,5},{5,4},{6,7},{7,6},{8,9},{9,8},{10,11... | collective-permute-start | bytes 3145736 | tf_op jit(solution)/shard_map/ppermute | solution.py:243
  35.6 0.1 pad_add_fusion.place
  35.7 2.5 %collective-permute-done.kvb_ref = bf16[4096,128]{1,0:T(8,128)(2,1)S(1)} collective-permute-done((bf16[4096,128]{1,0:T(8,128)(2,1)S(1)}, bf16[4096,128]{1,0:T(8,128)(2,1)S(1)}, u32[]{:S(2)}, u32[]{:S(2)}) %collective-permute-start) | collective-permute-done | bytes 1048608 | tf_op jit(solution)/shard_map/ppermute | solution.py:243
  38.3 0.0 copy-done
  38.3 0.0 copy-done.3
  38.3 0.0 copy-done.2
  38.3 10.4 %parts.1 = (bf16[4096,128]{1,0:T(8,128)(2,1)S(1)}, bf16[4096,128]{1,0:T(8,128)(2,1)S(1)}, bf16[2048,1280]{1,0:T(8,128)(2,1)S(1)}, bf16[2048,1280]{1,0:T(8,128)(2,1)S(1)}) custom-call(s32[3]{0:T(128)S(1)} %pad_add_fusion.place, s32[2,16]{1,0:T(2,128)S(1)} %bitcast.12, s32[10,32]{1,0:T(8,128)S(1)} %bitcast.10, bf16[256,1024]{1,0:T(8,128)(2,1)S(1)} %copy-done.2, ...), custom_call_target="tpu_custom_call" | custom-call | flops 2684354560 | bytes 6291456 | tf_op jit(solution)/shard_map/parts/pallas_call | solution.py:179
  48.7 2.0 %collective-permute-start.1 = (bf16[4096,128]{1,0:T(8,128)(2,1)S(1)}, bf16[4096,128]{1,0:T(8,128)(2,1)S(1)}, u32[]{:S(2)}, u32[]{:S(2)}) collective-permute-start(bf16[4096,128]{1,0:T(8,128)(2,1)S(1)} %get-tuple-element.14), channel_id=1, source_target_pairs={{0,1},{1,0},{2,3},{3,2},{4,5},{5,4},{6,7},{7,6},{8,9},{9,8},{10,11... | collective-permute-start | bytes 3145736 | tf_op jit(solution)/shard_map/ppermute | solution.py:247
  50.7 2.5 %collective-permute-done.1 = bf16[4096,128]{1,0:T(8,128)(2,1)S(1)} collective-permute-done((bf16[4096,128]{1,0:T(8,128)(2,1)S(1)}, bf16[4096,128]{1,0:T(8,128)(2,1)S(1)}, u32[]{:S(2)}, u32[]{:S(2)}) %collective-permute-start.1) | collective-permute-done | bytes 1048608 | tf_op jit(solution)/shard_map/ppermute | solution.py:247
  53.2 0.3 add_convert_fusion
  53.5 18.1 %all_to_all.11 = bf16[4,1024,128]{2,1,0:T(8,128)(2,1)S(1)} all-to-all(bf16[4,1024,128]{2,1,0:T(8,128)(2,1)S(1)} %bitcast.14), channel_id=1, replica_groups=mesh['dp'=4,'head'=8,'x'=4,'yh'=2,'core'=2] {'x'}, dimensions={0} | all-to-all | bytes 2097152 | tf_op jit(solution)/shard_map/all_to_all | solution.py:251
  71.6 0.1 convert_reduce_fusion
  71.8 2.2 %collective-permute-start.2 = (bf16[512,128]{1,0:T(8,128)(2,1)S(1)}, bf16[512,128]{1,0:T(8,128)(2,1)S(1)}, u32[]{:S(2)}, u32[]{:S(2)}) collective-permute-start(bf16[512,128]{1,0:T(8,128)(2,1)S(1)} %slice.35), channel_id=1, source_target_pairs={{0,2},{2,0},{1,3},{3,1},{4,6},{6,4},{5,7},{7,5},{8,10},{10,8},{9,1... | collective-permute-start | bytes 393224 | tf_op jit(solution)/shard_map/ppermute | solution.py:253
  73.9 5.1 %rows.1 = (bf16[256,1024]{1,0:T(8,128)(2,1)}, bf16[256,1024]{1,0:T(8,128)(2,1)}) custom-call(s32[3]{0:T(128)S(1)} %pad_add_fusion.place, s32[2,16]{1,0:T(2,128)S(1)} %bitcast.13, s32[10,32]{1,0:T(8,128)S(1)} %bitcast.11, bf16[2048,1280]{1,0:T(8,128)(2,1)S(1)} %get-tuple-element.17.p_ref, bf16[2048,1280]{1,0:T(8,128)(2,1)S(1)} %get-tuple-element.18.ds_ref, ...), custom_call_target="tpu_custom_call" | custom-call | flops 1342177280 | bytes 6291456 | tf_op jit(solution)/shard_map/rows/pallas_call | solution.py:211
  79.1 4.1 %collective-permute-done.2 = bf16[512,128]{1,0:T(8,128)(2,1)S(1)} collective-permute-done((bf16[512,128]{1,0:T(8,128)(2,1)S(1)}, bf16[512,128]{1,0:T(8,128)(2,1)S(1)}, u32[]{:S(2)}, u32[]{:S(2)}) %collective-permute-start.2) | collective-permute-done | bytes 131104 | tf_op jit(solution)/shard_map/ppermute | solution.py:253
  83.1 0.7 fusion
  (2 shorter events, 0.0 us)
Async XLA Ops:
  0.6 37.6 %copy-start = (s32[32,10]{0,1:T(8,128)S(1)}, s32[32,10]{0,1:T(8,128)}, u32[]{:S(2)}) copy-start(s32[32,10]{0,1:T(8,128)} %param.11) | copy-start | bytes 3844
  0.6 37.6 %copy-start.1 = (s32[16,2]{0,1:T(2,128)S(1)}, s32[16,2]{0,1:T(2,128)}, u32[]{:S(2)}) copy-start(s32[16,2]{0,1:T(2,128)} %param.10) | copy-start | bytes 388
  0.7 37.6 %copy-start.3 = (bf16[256,1024]{1,0:T(8,128)(2,1)S(1)}, bf16[256,1024]{1,0:T(8,128)(2,1)}, u32[]{:S(2)}) copy-start(bf16[256,1024]{1,0:T(8,128)(2,1)} %g_ref.1) | copy-start | bytes 1572868
  0.7 37.6 %copy-start.2 = (bf16[256,1024]{1,0:T(8,128)(2,1)S(1)}, bf16[256,1024]{1,0:T(8,128)(2,1)}, u32[]{:S(2)}) copy-start(bf16[256,1024]{1,0:T(8,128)(2,1)} %q_ref.1) | copy-start | bytes 1572868
  33.7 4.5 %collective-permute-start = (bf16[4096,128]{1,0:T(8,128)(2,1)S(1)}, bf16[4096,128]{1,0:T(8,128)(2,1)S(1)}, u32[]{:S(2)}, u32[]{:S(2)}) collective-permute-start(bf16[4096,128]{1,0:T(8,128)(2,1)S(1)} %bitcast.7), channel_id=1, source_target_pairs={{0,1},{1,0},{2,3},{3,2},{4,5},{5,4},{6,7},{7,6},{8,9},{9,8},{10,11... | collective-permute-start | bytes 3145736 | tf_op jit(solution)/shard_map/ppermute | solution.py:243
  48.7 4.6 %collective-permute-start.1 = (bf16[4096,128]{1,0:T(8,128)(2,1)S(1)}, bf16[4096,128]{1,0:T(8,128)(2,1)S(1)}, u32[]{:S(2)}, u32[]{:S(2)}) collective-permute-start(bf16[4096,128]{1,0:T(8,128)(2,1)S(1)} %get-tuple-element.14), channel_id=1, source_target_pairs={{0,1},{1,0},{2,3},{3,2},{4,5},{5,4},{6,7},{7,6},{8,9},{9,8},{10,11... | collective-permute-start | bytes 3145736 | tf_op jit(solution)/shard_map/ppermute | solution.py:247
  71.8 11.4 %collective-permute-start.2 = (bf16[512,128]{1,0:T(8,128)(2,1)S(1)}, bf16[512,128]{1,0:T(8,128)(2,1)S(1)}, u32[]{:S(2)}, u32[]{:S(2)}) collective-permute-start(bf16[512,128]{1,0:T(8,128)(2,1)S(1)} %slice.35), channel_id=1, source_target_pairs={{0,2},{2,0},{1,3},{3,1},{4,6},{6,4},{5,7},{7,5},{8,10},{10,8},{9,1... | collective-permute-start | bytes 393224 | tf_op jit(solution)/shard_map/ppermute | solution.py:253
